TPU v7x, 256 devices: a whole 4x4x8 slice. The times are simulated.
256 devices in a mesh: seq: 64 (over z, y, core), batch: 4 (over x).
Axes of the slice: x: 4, y: 4, z: 8, core: 2. Of those that a mesh axis runs over, the one named last changes fastest.
Arguments:
- queries: bfloat16 [4, 32768, 16, 128], P('batch', 'seq'), may hold values from -5 to 5
- keys: bfloat16 [4, 32768, 16, 128], P('batch', 'seq'), may hold values from -5 to 5
- values: bfloat16 [4, 32768, 16, 128], P('batch', 'seq'), may hold values from -5 to 5
- keep_count: int32 [4, 16, 256], P('batch'), may hold values from 0 to 128
- query_map: bfloat16 [16, 128, 8], replicated, may hold values from -0.5 to 0.5
- key_map: bfloat16 [16, 128, 8], replicated, may hold values from -0.5 to 0.5
- cotangent: bfloat16 [4, 32768, 16, 128], P('batch', 'seq'), may hold values from -5 to 5
Outputs:
- attended: bfloat16 [4, 32768, 16, 128], P('batch', 'seq')
- grad_query_map: float32 [16, 128, 8], replicated
- grad_key_map: float32 [16, 128, 8], replicated
All inputs are finite; a program needn't handle non-finite values.
Results may differ from a plain program's by a relative error of at most 0.0035.
Values may be sent and summed in bfloat16 or wider, within the bound.
A program may use at most 128 MiB of HBM per device.

v0:
```python
import functools
import math

import jax
import jax.numpy as jnp
from jax import lax
from jax.experimental import pallas as pl
from jax.experimental.pallas import tpu as pltpu
from jax.sharding import Mesh
from jax.sharding import PartitionSpec as P

TILE = 128
SHIFT = 1.5
LOG2E = math.log2(math.e)
Z_AXIS, Y_AXIS, C_AXIS, X_AXIS = "seq_0", "seq_1", "seq_2", "batch"
SEQ = (Z_AXIS, Y_AXIS, C_AXIS)
F32, BF16 = jnp.float32, jnp.bfloat16
BLOCK = 16


def dot_nn(a, b):
    return lax.dot_general(a, b, (((1,), (0,)), ((), ())), preferred_element_type=F32)


def dot_nt(a, b):
    return lax.dot_general(a, b, (((1,), (1,)), ((), ())), preferred_element_type=F32)


def dot_tn(a, b):
    return lax.dot_general(a, b, (((0,), (0,)), ((), ())), preferred_element_type=F32)


def halves(x):
    high = x.astype(BF16).astype(F32)
    return high, x - high


def stacked(x):
    return jnp.concatenate(halves(x), 0).astype(BF16)


def folded(x):
    half = x.shape[0] // 2
    return x[:half] + x[half:]


def feature(pre):
    small = jnp.exp(-jnp.abs(pre))
    inverse = 1.0 / (1.0 + small)
    return jnp.maximum(pre, 0.0) + jnp.log1p(small), jnp.where(pre >= 0.0, inverse, small * inverse)


def remote(source, target, send, receive, device):
    return pltpu.make_async_remote_copy(
        src_ref=source,
        dst_ref=target,
        send_sem=send,
        recv_sem=receive,
        device_id=device,
        device_id_type=pl.DeviceIdType.MESH,
    )


def kernel(
    sizes,
    q_hbm, k_hbm, v_hbm, c_hbm, count_ref, wq_ref, wk_ref,
    out_hbm, gq_ref, gk_ref,
    q_raw, k_raw, v_raw, c_raw, halo_raw, o_raw,
    q_rows, k_rows, v_rows, c_rows, o_rows, numer,
    feat_q, slope_q, feat_k, slope_k, kept_lane, count_lane,
    state_local, norm_local, u_local, row_data, g_rows, gpre_q, d_state, d_norm, gk_local,
    p_send, p_land, p_total, p_far, p_out, p_back,
    s_send, s_land, s_total, s_far, s_out, s_back,
    rq_send, rq_land, rq_z, rq_zland, rq_x, rq_xland, rq_sum,
    rk_send, rk_land, rk_z, rk_zland, rk_x, rk_xland, rk_sum,
    acc,
    load_sem, store_sem, halo_sems, p_sems, s_sems, rq_sems, rk_sems,
):
    nz, ny, nc, nx = sizes
    group = ny * nc
    devices = nz * group
    tokens, heads, width = q_raw.shape
    tiles = tokens // TILE
    own = heads // group
    lanes = lax.broadcasted_iota(jnp.int32, (8, TILE), 1)
    z, y, c, x = (lax.axis_index(a) for a in (Z_AXIS, Y_AXIS, C_AXIS, X_AXIS))
    me = y * nc + c
    index = z * group + me

    def peer(s):
        return {Y_AXIS: s // nc, C_AXIS: s % nc}

    def place(i):
        return {Z_AXIS: i // group, Y_AXIS: (i // nc) % ny, C_AXIS: i % nc}

    after = place((index + 1) % devices)
    before = place((index + devices - 1) % devices)

    barrier = pltpu.get_barrier_semaphore()

    def greet(device):
        pl.semaphore_signal(barrier, inc=1, device_id=device, device_id_type=pl.DeviceIdType.MESH)

    greet(after)
    greet(before)
    for k in range(1, group):
        greet(peer((me + k) % group))
    for k in range(1, nz):
        greet({Z_AXIS: (z + k) % nz})
    for k in range(1, nx):
        greet({X_AXIS: (x + k) % nx})

    sources = (k_hbm, v_hbm, c_hbm, q_hbm)
    raws = (k_raw, v_raw, c_raw, q_raw)

    def load(a, t):
        rows = pl.ds(t * TILE, TILE)
        return pltpu.make_async_copy(sources[a].at[rows], raws[a].at[rows], load_sem.at[a * tiles + t])

    for a in range(4):
        for t in range(tiles):
            load(a, t).start()

    def by_head(raw, rows, first, target, count):
        def step(b, _):
            block = raw[pl.ds(rows + b * BLOCK, BLOCK)]
            target[:, pl.ds(first + b * BLOCK, BLOCK), :] = jnp.swapaxes(block, 0, 1)
            return 0

        lax.fori_loop(0, count // BLOCK, step, 0, unroll=4)

    for t in range(tiles):
        load(0, t).wait()
        by_head(k_raw, t * TILE, (t + 1) * TILE, k_rows, TILE)
        load(1, t).wait()
        by_head(v_raw, t * TILE, (t + 1) * TILE, v_rows, TILE)

    counts = count_ref[...]
    which = lax.broadcasted_iota(jnp.int32, counts.shape, 1)
    lane16 = lax.broadcasted_iota(jnp.int32, (heads, TILE), 1)
    for e in range(tiles + 1):
        picked = jnp.sum(jnp.where(which == index * tiles + (e - 1), counts, 0), 1, keepdims=True)
        spread = jnp.broadcast_to(picked, (heads, TILE))
        kept = (lane16 < spread).astype(F32)
        for h in range(heads):
            count_lane[e, h] = jnp.broadcast_to(spread[h : h + 1], (8, TILE))
            kept_lane[h, :, e * TILE : (e + 1) * TILE] = jnp.broadcast_to(kept[h : h + 1], (8, TILE))

    pl.semaphore_wait(barrier, 2 + group - 1 + nz - 1 + nx - 1)
    halo_from = pl.ds(tokens - TILE, TILE)
    halo_copies = [
        remote(k_hbm.at[halo_from], halo_raw.at[0], halo_sems.at[0], halo_sems.at[2], after),
        remote(v_hbm.at[halo_from], halo_raw.at[1], halo_sems.at[1], halo_sems.at[3], after),
    ]
    for copy in halo_copies:
        copy.start()

    def scatter(buffer, land, sems, s):
        return remote(buffer.at[s], land.at[me], sems.at[s], sems.at[group + me], peer(s))

    def arrival(buffer, land, sems, s):
        return remote(buffer.at[s], land.at[s], sems.at[s], sems.at[group + s], peer(s))

    def share(buffer, land, sems, s):
        return remote(buffer, land.at[me], sems.at[s], sems.at[group + me], peer(s))

    def share_arrival(buffer, land, sems, s):
        return remote(buffer, land.at[s], sems.at[s], sems.at[group + s], peer(s))

    def z_copy(buffer, land, sems, t):
        return remote(buffer, land.at[z], sems.at[t], sems.at[nz + z], {Z_AXIS: t})

    def z_arrival(buffer, land, sems, t):
        return remote(buffer, land.at[t], sems.at[t], sems.at[nz + t], {Z_AXIS: t})

    def x_copy(buffer, land, sems, t):
        return remote(buffer, land.at[x], sems.at[t], sems.at[nx + x], {X_AXIS: t})

    def x_arrival(buffer, land, sems, t):
        return remote(buffer, land.at[t], sems.at[t], sems.at[nx + t], {X_AXIS: t})

    def others(step, count=group, here=None):
        here = me if here is None else here

        def one(k, _):
            step((here + 1 + k) % count)
            return 0

        lax.fori_loop(0, count - 1, one, 0)

    def owner_slice(pieces, norms):
        low = jnp.where(lanes < TILE // 2, norms[0], norms[1])
        return jnp.concatenate([*pieces, low], 0)

    def norm_of(tile, i):
        turned = pltpu.roll(tile, TILE // 2, 1)
        return jnp.where(lanes < TILE // 2, *((tile, turned) if i == 0 else (turned, tile)))

    own_rows = pl.ds(TILE, tokens)

    def state_slice(o):
        pieces, norms = [], []
        for i in range(own):
            h = o * own + i
            feat, slope = feature(dot_nt(wk_ref[h], k_rows[h, own_rows, :]) - SHIFT)
            feat_k[h, :, TILE:] = feat
            slope_k[h, :, TILE:] = slope
            pieces.append(folded(dot_nn(stacked(feat), v_rows[h, own_rows, :])))
            norms.append(jnp.sum(feat, 1, keepdims=True))
        return owner_slice(pieces, norms)

    def state_send(o):
        p_send[o] = state_slice(o)
        scatter(p_send, p_land, p_sems[0], o).start()

    others(state_send)
    p_land[me] = state_slice(me)

    def query_features(h, _):
        feat, slope = feature(dot_nt(wq_ref[h], q_rows[h]) - SHIFT)
        feat_q[h] = feat
        slope_q[h] = slope
        return 0

    for t in range(tiles):
        load(2, t).wait()
        by_head(c_raw, t * TILE, t * TILE, c_rows, TILE)
        load(3, t).wait()
        by_head(q_raw, t * TILE, t * TILE, q_rows, TILE)
    lax.fori_loop(0, heads, query_features, 0)

    def local_terms(h, j, state, norm):
        cols = slice(j * TILE, (j + 1) * TILE)
        state_local[h, j] = state
        norm_local[h, :, cols] = jnp.broadcast_to(norm, (8, TILE))
        u = folded(dot_nt(stacked(state), c_rows[h, cols, :]))
        u_local[h, :, cols] = u
        fq = feat_q[h, :, cols]
        row_data[h, 3:4, cols] = jnp.sum(fq * norm, 0, keepdims=True)
        row_data[h, 4:5, cols] = jnp.sum(fq * u, 0, keepdims=True)

    def local_states(h, _):
        full, full_norm, out, out_norm = [], [], [], []
        for i in range(tiles - 1):
            cols = slice((i + 1) * TILE, (i + 2) * TILE)
            feat = feat_k[h, :, cols]
            gone = feat * (1.0 - kept_lane[h, :, cols])
            both = jnp.concatenate([*halves(feat), *halves(gone)], 0).astype(BF16)
            result = dot_nn(both, v_rows[h, cols, :])
            full.append(folded(result[:16]))
            out.append(folded(result[16:]))
            full_norm.append(jnp.sum(feat, 1, keepdims=True))
            out_norm.append(jnp.sum(gone, 1, keepdims=True))
        for j in range(1, tiles):
            local_terms(
                h, j, sum(full[: j - 1], out[j - 1]), sum(full_norm[: j - 1], out_norm[j - 1])
            )
        return 0

    scale2 = LOG2E / math.sqrt(width)
    key_at = lax.broadcasted_iota(jnp.int32, (TILE, TILE), 0)
    causal = key_at <= lax.broadcasted_iota(jnp.int32, (TILE, TILE), 1)

    def sparse(h, j):
        cols = slice(j * TILE, (j + 1) * TILE)
        window = slice(j * TILE, (j + 2) * TILE)
        v_window = v_rows[h, window, :]
        scores = dot_nt(k_rows[h, window, :], q_rows[h, cols, :])
        live = key_at < count_lane[j, h, 0:1, :]
        near = jnp.where(live, scores[:TILE], -1e30)
        here = jnp.where(causal, scores[TILE:], -1e30)
        top = jnp.maximum(jnp.max(near, 0, keepdims=True), jnp.max(here, 0, keepdims=True))
        shift = top * scale2
        masked = jnp.concatenate([near, here], 0)
        weights = jnp.exp2(masked * scale2 - shift)
        rounded = weights.astype(BF16)
        numer[h, cols, :] = dot_tn(rounded, v_window)
        along = dot_nt(v_window, c_rows[h, cols, :])
        row_data[h, 0:1, cols] = jnp.exp2(-shift)
        row_data[h, 1:2, cols] = jnp.sum(weights, 0, keepdims=True)
        row_data[h, 2:3, cols] = jnp.sum(rounded.astype(F32) * along, 0, keepdims=True)

    def sparse_tile(j):
        def one(h, _):
            sparse(h, j)
            return 0

        lax.fori_loop(0, heads, one, 0)

    others(lambda s: arrival(p_send, p_land, p_sems[0], s).wait_recv())
    p_total[...] = sum(p_land[s] for s in range(1, group)) + p_land[0]
    for t in range(1, nz):
        @pl.when(t > z)
        def _():
            z_copy(p_total, p_far, p_sems[1], t).start()

    lax.fori_loop(0, heads, local_states, 0)
    sparse_tile(1)
    sparse_tile(2)

    acc[...] = jnp.zeros_like(acc)
    for t in range(nz - 1):
        @pl.when(t < z)
        def _():
            z_arrival(p_total, p_far, p_sems[1], t).wait_recv()
            acc[...] += p_far[t]

    running = acc[...]
    for s in range(group):
        p_out[s] = running
        running = running + p_land[s]
    others(lambda s: scatter(p_out, p_back, p_sems[2], s).start())
    p_back[me] = p_out[me]

    sparse_tile(3)

    for copy in halo_copies:
        copy.wait_recv()
    by_head(halo_raw.at[0], 0, 0, k_rows, TILE)
    by_head(halo_raw.at[1], 0, 0, v_rows, TILE)

    def halo_head(h, _):
        feat, slope = feature(dot_nt(wk_ref[h], k_rows[h, :TILE, :]) - SHIFT)
        slope_k[h, :, :TILE] = slope
        held = feat * kept_lane[h, :, :TILE]
        state = folded(dot_nn(stacked(held), v_rows[h, :TILE, :]))
        local_terms(h, 0, -state, -jnp.sum(held, 1, keepdims=True))
        sparse(h, 0)
        return 0

    lax.fori_loop(0, heads, halo_head, 0)

    def d_slice(o):
        pieces, norms = [], []
        back = p_back[o]
        for i in range(own):
            h = o * own + i
            far = back[i * 8 : (i + 1) * 8]
            far_norm = jnp.concatenate([norm_of(back[own * 8 :], i)] * tiles, 1)
            fq = feat_q[h]
            u_far = folded(dot_nt(stacked(far), c_rows[h]))
            decay = row_data[h, 0:1, :]
            kd = row_data[h, 3:4, :] + jnp.sum(fq * far_norm, 0, keepdims=True)
            cu = row_data[h, 4:5, :] + jnp.sum(fq * u_far, 0, keepdims=True)
            inverse = 1.0 / (row_data[h, 1:2, :] + decay * kd)
            share_of = decay * inverse
            g = fq * share_of
            g_den = -share_of * ((row_data[h, 2:3, :] + decay * cu) * inverse)
            g_rows[h] = g
            row_data[h, 5:6, :] = inverse
            gpre_q[h] = (
                share_of * (u_local[h] + u_far) + g_den * (norm_local[h] + far_norm)
            ) * slope_q[h]
            weighted = fq * g_den
            total, total_norm = None, None
            for j in range(tiles):
                cols = slice(j * TILE, (j + 1) * TILE)
                piece = folded(dot_nn(stacked(g[:, cols]), c_rows[h, cols, :]))
                norm = jnp.sum(weighted[:, cols], 1, keepdims=True)
                d_state[h, j] = piece
                d_norm[h, j] = jnp.broadcast_to(norm, (8, TILE))
                total = piece if j == 0 else total + piece
                total_norm = norm if j == 0 else total_norm + norm
            pieces.append(total)
            norms.append(total_norm)
        return owner_slice(pieces, norms)

    def d_send(o):
        arrival(p_out, p_back, p_sems[2], o).wait_recv()
        s_send[o] = d_slice(o)
        scatter(s_send, s_land, s_sems[0], o).start()

    others(d_send)
    s_land[me] = d_slice(me)

    def query_slice(o):
        pieces = []
        for i in range(own):
            h = o * own + i
            pieces.append(folded(dot_nn(stacked(gpre_q[h]), q_rows[h])))
        return jnp.concatenate(pieces, 0)

    def query_send(o):
        rq_send[o] = query_slice(o)
        scatter(rq_send, rq_land, rq_sems[0], o).start()

    others(query_send)
    rq_land[me] = query_slice(me)

    def key_local(h, _):
        parts = []
        for e in range(tiles):
            cols = slice(e * TILE, (e + 1) * TILE)
            v_tile = v_rows[h, cols, :]
            kept = kept_lane[h, :, cols]
            if e == 0:
                grad = -kept * (folded(dot_nt(stacked(d_state[h, 0]), v_tile)) + d_norm[h, 0])
            else:
                near, near_norm = d_state[h, e], d_norm[h, e]
                if e + 1 < tiles:
                    full = sum([d_state[h, j] for j in range(e + 2, tiles)], d_state[h, e + 1])
                    full_norm = sum([d_norm[h, j] for j in range(e + 2, tiles)], d_norm[h, e + 1])
                    both = jnp.concatenate([*halves(near), *halves(full)], 0).astype(BF16)
                    result = dot_nt(both, v_tile)
                    grad = (1.0 - kept) * (folded(result[:16]) + near_norm)
                    grad = grad + (folded(result[16:]) + full_norm)
                else:
                    grad = (1.0 - kept) * (folded(dot_nt(stacked(near), v_tile)) + near_norm)
            parts.append(grad * slope_k[h, :, cols])
        gk_local[h] = folded(dot_nn(stacked(jnp.concatenate(parts, 1)), k_rows[h, :tokens, :]))
        return 0

    sub = lax.broadcasted_iota(jnp.int32, (8, TILE), 0)

    def outputs(h, o, i):
        back = p_back[o]
        far = back[i * 8 : (i + 1) * 8]
        for j in range(tiles):
            cols = slice(j * TILE, (j + 1) * TILE)
            high, low = halves(far + state_local[h, j])
            g_high, g_low = halves(g_rows[h, :, cols])
            first, rest = halves(row_data[h, 5:6, cols])
            second, third = halves(rest)
            inverse = jnp.where(sub == 0, first, jnp.where(sub == 1, second, third))
            inverse = jnp.where(sub < 3, inverse, 0.0)
            left = jnp.concatenate([g_high, g_low, g_high, inverse], 0).astype(BF16)
            zeros, ones = jnp.zeros((8, TILE), F32), jnp.ones((8, TILE), F32)
            right = jnp.concatenate(
                [
                    jnp.concatenate([high, high, low, zeros], 0),
                    jnp.concatenate([zeros, zeros, zeros, ones], 0),
                ],
                1,
            ).astype(BF16)
            both = dot_tn(left, right)
            result = numer[h, cols, :] * both[:, TILE:] + both[:, :TILE]
            o_rows[h, cols, :] = result.astype(BF16)

    def outputs_owner(o, _):
        for i in range(own):
            outputs(o * own + i, o, i)
        return 0

    lax.fori_loop(0, heads, key_local, 0)

    others(lambda s: arrival(s_send, s_land, s_sems[0], s).wait_recv())
    s_total[...] = sum(s_land[s] for s in range(1, group)) + s_land[0]
    for t in range(nz - 1):
        @pl.when(t < z)
        def _():
            z_copy(s_total, s_far, s_sems[1], t).start()

    others(lambda s: arrival(rq_send, rq_land, rq_sems[0], s).wait_recv())
    rq_z[...] = sum(rq_land[s] for s in range(1, group)) + rq_land[0]
    others(lambda t: z_copy(rq_z, rq_zland, rq_sems[1], t).start(), nz, z)
    rq_zland[z] = rq_z[...]

    lax.fori_loop(0, group, outputs_owner, 0)

    acc[...] = jnp.zeros_like(acc)
    for t in range(1, nz):
        @pl.when(t > z)
        def _():
            z_arrival(s_total, s_far, s_sems[1], t).wait_recv()
            acc[...] += s_far[t]

    running = acc[...]
    for s in reversed(range(group)):
        s_out[s] = running
        running = running + s_land[s]
    others(lambda s: scatter(s_out, s_back, s_sems[2], s).start())
    s_back[me] = s_out[me]

    others(lambda t: z_arrival(rq_z, rq_zland, rq_sems[1], t).wait_recv(), nz, z)
    rq_x[...] = sum(rq_zland[t] for t in range(1, nz)) + rq_zland[0]
    others(lambda t: x_copy(rq_x, rq_xland, rq_sems[2], t).start(), nx, x)
    rq_xland[x] = rq_x[...]

    def by_position(b, _):
        block = o_rows[:, pl.ds(b * BLOCK, BLOCK), :]
        o_raw[pl.ds(b * BLOCK, BLOCK)] = jnp.swapaxes(block, 0, 1)
        return 0

    lax.fori_loop(0, tokens // BLOCK, by_position, 0, unroll=4)
    store = pltpu.make_async_copy(o_raw, out_hbm, store_sem)
    store.start()

    def key_slice(o):
        pieces = []
        back = s_back[o]
        for i in range(own):
            h = o * own + i
            far_norm = jnp.concatenate([norm_of(back[own * 8 :], i)] * tiles, 1)
            grad = folded(dot_nt(stacked(back[i * 8 : (i + 1) * 8]), v_rows[h, own_rows, :]))
            grad = (grad + far_norm) * slope_k[h, :, TILE:]
            pieces.append(gk_local[h] + folded(dot_nn(stacked(grad), k_rows[h, own_rows, :])))
        return jnp.concatenate(pieces, 0)

    def key_send(o):
        arrival(s_out, s_back, s_sems[2], o).wait_recv()
        rk_send[o] = key_slice(o)
        scatter(rk_send, rk_land, rk_sems[0], o).start()

    others(key_send)
    rk_land[me] = key_slice(me)

    others(lambda t: x_arrival(rq_x, rq_xland, rq_sems[2], t).wait_recv(), nx, x)
    rq_sum[...] = sum(rq_xland[t] for t in range(1, nx)) + rq_xland[0]
    others(lambda s: share(rq_sum, gq_ref, rq_sems[3], s).start())
    gq_ref[me] = rq_sum[...]

    others(lambda s: arrival(rk_send, rk_land, rk_sems[0], s).wait_recv())
    rk_z[...] = sum(rk_land[s] for s in range(1, group)) + rk_land[0]
    others(lambda t: z_copy(rk_z, rk_zland, rk_sems[1], t).start(), nz, z)
    rk_zland[z] = rk_z[...]
    others(lambda t: z_arrival(rk_z, rk_zland, rk_sems[1], t).wait_recv(), nz, z)
    rk_x[...] = sum(rk_zland[t] for t in range(1, nz)) + rk_zland[0]
    others(lambda t: x_copy(rk_x, rk_xland, rk_sems[2], t).start(), nx, x)
    rk_xland[x] = rk_x[...]
    others(lambda t: x_arrival(rk_x, rk_xland, rk_sems[2], t).wait_recv(), nx, x)
    rk_sum[...] = sum(rk_xland[t] for t in range(1, nx)) + rk_xland[0]
    others(lambda s: share(rk_sum, gk_ref, rk_sems[3], s).start())
    gk_ref[me] = rk_sum[...]

    for copy in halo_copies:
        copy.wait_send()
    others(lambda s: scatter(p_send, p_land, p_sems[0], s).wait_send())
    others(lambda s: scatter(p_out, p_back, p_sems[2], s).wait_send())
    others(lambda s: scatter(s_send, s_land, s_sems[0], s).wait_send())
    others(lambda s: scatter(s_out, s_back, s_sems[2], s).wait_send())
    for t in range(nz):
        @pl.when(t > z)
        def _():
            z_copy(p_total, p_far, p_sems[1], t).wait_send()

        @pl.when(t < z)
        def _():
            z_copy(s_total, s_far, s_sems[1], t).wait_send()
    for send, land, zs, zland, xs, xland, total, grad, sems in (
        (rq_send, rq_land, rq_z, rq_zland, rq_x, rq_xland, rq_sum, gq_ref, rq_sems),
        (rk_send, rk_land, rk_z, rk_zland, rk_x, rk_xland, rk_sum, gk_ref, rk_sems),
    ):
        others(lambda s: scatter(send, land, sems[0], s).wait_send())
        others(lambda t: z_copy(zs, zland, sems[1], t).wait_send(), nz, z)
        others(lambda t: x_copy(xs, xland, sems[2], t).wait_send(), nx, x)
        others(lambda s: share(total, grad, sems[3], s).wait_send())
        others(lambda s: share_arrival(total, grad, sems[3], s).wait_recv())
    store.wait()


def body(queries, keys, values, keep_count, query_map, key_map, cotangent):
    _, tokens, heads, width = queries.shape
    rank = query_map.shape[2]
    tiles = tokens // TILE
    sizes = tuple(lax.axis_size(a) for a in (Z_AXIS, Y_AXIS, C_AXIS, X_AXIS))
    nz, ny, nc, nx = sizes
    group = ny * nc
    own = heads // group
    ext = tokens + TILE
    part = (own * rank, width)
    slab = (own * rank + 8, width)
    dma = pltpu.SemaphoreType.DMA

    def vmem(shape, dtype=F32):
        return pltpu.VMEM(shape, dtype)

    def sums():
        return [
            vmem((group, *part)), vmem((group, *part)), vmem(part), vmem((nz, *part)),
            vmem(part), vmem((nx, *part)), vmem(part),
        ]

    def scans():
        return [
            vmem((group, *slab)), vmem((group, *slab)), vmem(slab), vmem((nz, *slab)),
            vmem((group, *slab)), vmem((group, *slab)),
        ]

    raw = (tokens, heads, width)
    lane_rows = (heads, rank, tokens)
    scratch = [
        *[vmem(raw, BF16)] * 4, vmem((2, TILE, heads, width), BF16), vmem(raw, BF16),
        vmem((heads, tokens, width), BF16), vmem((heads, ext, width), BF16),
        vmem((heads, ext, width), BF16), vmem((heads, tokens, width), BF16),
        vmem((heads, tokens, width), BF16), vmem((heads, tokens, width)),
        vmem(lane_rows), vmem(lane_rows), vmem((heads, rank, ext)), vmem((heads, rank, ext)),
        vmem((heads, 8, ext)), vmem((tiles + 1, heads, 8, TILE), jnp.int32),
        vmem((heads, tiles, rank, width)), vmem(lane_rows), vmem(lane_rows),
        vmem((heads, 8, tokens)), vmem(lane_rows), vmem(lane_rows),
        vmem((heads, tiles, rank, width)), vmem((heads, tiles, rank, width)),
        vmem((heads, rank, width)),
        *scans(), *scans(), *sums(), *sums(), vmem(slab),
        dma((4 * tiles,)), dma, dma((4,)),
        [dma((2 * group,)), dma((2 * nz,)), dma((2 * group,))],
        [dma((2 * group,)), dma((2 * nz,)), dma((2 * group,))],
        [dma((2 * group,)), dma((2 * nz,)), dma((2 * nx,)), dma((2 * group,))],
        [dma((2 * group,)), dma((2 * nz,)), dma((2 * nx,)), dma((2 * group,))],
    ]
    anywhere = pl.BlockSpec(memory_space=pl.ANY)
    here = pl.BlockSpec(memory_space=pltpu.VMEM)
    grad = jax.ShapeDtypeStruct((group, *part), F32)
    out, grad_q, grad_k = pl.pallas_call(
        functools.partial(kernel, sizes),
        out_shape=(jax.ShapeDtypeStruct(raw, BF16), grad, grad),
        in_specs=[anywhere] * 4 + [here] * 3,
        out_specs=(anywhere, here, here),
        scratch_shapes=scratch,
        compiler_params=pltpu.CompilerParams(
            collective_id=0, has_side_effects=True, vmem_limit_bytes=60 * 2**20
        ),
        name="less_step",
    )(
        queries[0], keys[0], values[0], cotangent[0], keep_count[0],
        query_map.transpose(0, 2, 1), key_map.transpose(0, 2, 1),
    )

    def map_grad(g):
        return g.reshape(heads, rank, width).transpose(0, 2, 1)

    return (out[None], map_grad(grad_q), map_grad(grad_k))


def solution(mesh):
    chips, last = mesh.shape["seq"], mesh.shape["batch"]
    torus = Mesh(mesh.devices.reshape(chips // 8, 4, 2, last), (*SEQ, X_AXIS))
    rows = P(X_AXIS, SEQ, None, None)
    return jax.shard_map(
        body,
        mesh=torus,
        in_specs=(rows, rows, rows, P(X_AXIS, None, None), P(), P(), rows),
        out_specs=(rows, P(), P()),
        check_vma=False,
    )
```

profile of v0, /device:TPU:1, one launch (start us, length us, event | category | flops | bytes accessed | tf_op | source)
XLA Modules:
  0.0 105.0 jit_solution(17437976068477133422)
XLA Ops:
  0.6 99.8 %less_step.1 = (bf16[512,16,128]{2,1,0:T(8,128)(2,1)}, f32[8,16,128]{2,1,0:T(8,128)}, f32[8,16,128]{2,1,0:T(8,128)}) custom-call(bf16[512,16,128]{2,1,0:T(8,128)(2,1)} %bitcast.15, bf16[512,16,128]{2,1,0:T(8,128)(2,1)} %bitcast.16, bf16[512,16,128]{2,1,0:T(8,128)(2,1)} %bitcast.17, bf16[512,16,128]{2,1,0:T(8,128)(2,1)} %bitcast.18, s32[16,256]{1,0:T(8,128)} %bitcast.23, ...), custom_call_target="tpu_custom_call" | custom-call | tf_op jit(solution)/shard_map/less_step/pallas_call | solution.py:602
  100.4 0.0 copy-start.1
  100.4 0.0 copy-start
  100.4 3.3 %copy.13 = bf16[1,512,16,128]{3,2,1,0:T(8,128)(2,1)} copy(bf16[1,512,16,128]{3,2,1,0:T(8,128)(2,1)} %bitcast.14) | data formatting | bytes 4194304
  103.7 0.0 copy-done.1
  103.7 0.6 copy.14
  104.4 0.0 copy-done
  104.4 0.6 copy.15
Async XLA Ops:
  100.4 3.3 %copy-start.1 = (f32[8,16,128]{2,1,0:T(8,128)S(1)}, f32[8,16,128]{2,1,0:T(8,128)}, u32[]{:S(2)}) copy-start(f32[8,16,128]{2,1,0:T(8,128)} %get-tuple-element.7) | copy-start | bytes 196612
  100.4 3.9 %copy-start = (f32[8,16,128]{2,1,0:T(8,128)S(1)}, f32[8,16,128]{2,1,0:T(8,128)}, u32[]{:S(2)}) copy-start(f32[8,16,128]{2,1,0:T(8,128)} %get-tuple-element.8) | copy-start | bytes 196612
where the time goes:
time: 105 us
  Pallas kernels  99.8 us (95%)
  local copies, waits for them, and re-layouts  4.57 us (4%)
    pallas_call x1, Pallas kernels, body(): pl.pallas_call(functools.partial(kernel, sizes), out_shape=(jax.ShapeDtyp...  99.8 us
    unnamed x7, local copies, waits for them, and re-layouts  4.57 us

commit v1 on v0

--- a/solution.py
+++ b/solution.py
@@ -65,10 +65,10 @@
     sizes,
     q_hbm, k_hbm, v_hbm, c_hbm, count_ref, wq_ref, wk_ref,
     out_hbm, gq_ref, gk_ref,
-    q_raw, k_raw, v_raw, c_raw, halo_raw, o_raw,
-    q_rows, k_rows, v_rows, c_rows, o_rows, numer,
+    q_raw, k_raw, v_raw, c_raw, halo_raw,
+    q_rows, k_rows, v_rows, c_rows, o_rows, weight_rows,
     feat_q, slope_q, feat_k, slope_k, kept_lane, count_lane,
-    state_local, norm_local, u_local, row_data, g_rows, gpre_q, d_state, d_norm, gk_local,
+    state_local, norm_local, u_local, row_data, inverse_rows, g_rows, gpre_q, d_state, d_norm, gk_local,
     p_send, p_land, p_total, p_far, p_out, p_back,
     s_send, s_land, s_total, s_far, s_out, s_back,
     rq_send, rq_land, rq_z, rq_zland, rq_x, rq_xland, rq_sum,
@@ -132,6 +132,14 @@
     for t in range(tiles):
         load(0, t).wait()
         by_head(k_raw, t * TILE, (t + 1) * TILE, k_rows, TILE)
+    pl.semaphore_wait(barrier, 2 + group - 1 + nz - 1 + nx - 1)
+    halo_from = pl.ds(tokens - TILE, TILE)
+    halo_copies = [
+        remote(k_hbm.at[halo_from], halo_raw.at[0], halo_sems.at[0], halo_sems.at[2], after),
+        remote(v_hbm.at[halo_from], halo_raw.at[1], halo_sems.at[1], halo_sems.at[3], after),
+    ]
+    halo_copies[0].start()
+    for t in range(tiles):
         load(1, t).wait()
         by_head(v_raw, t * TILE, (t + 1) * TILE, v_rows, TILE)
 
@@ -146,15 +154,6 @@
             count_lane[e, h] = jnp.broadcast_to(spread[h : h + 1], (8, TILE))
             kept_lane[h, :, e * TILE : (e + 1) * TILE] = jnp.broadcast_to(kept[h : h + 1], (8, TILE))
 
-    pl.semaphore_wait(barrier, 2 + group - 1 + nz - 1 + nx - 1)
-    halo_from = pl.ds(tokens - TILE, TILE)
-    halo_copies = [
-        remote(k_hbm.at[halo_from], halo_raw.at[0], halo_sems.at[0], halo_sems.at[2], after),
-        remote(v_hbm.at[halo_from], halo_raw.at[1], halo_sems.at[1], halo_sems.at[3], after),
-    ]
-    for copy in halo_copies:
-        copy.start()
-
     def scatter(buffer, land, sems, s):
         return remote(buffer.at[s], land.at[me], sems.at[s], sems.at[group + me], peer(s))
 
@@ -181,12 +180,26 @@
 
     def others(step, count=group, here=None):
         here = me if here is None else here
-
+        for k in sorted(range(1, count), key=lambda k: -min(k, count - k)):
+            step((here + k) % count)
+
+    def by_owner(compute, buffer, land, sems, ready=None):
         def one(k, _):
-            step((here + 1 + k) % count)
+            pair = [(me + group // 2 - k) % group, (me + group // 2 + 1 + k) % group]
+            if ready is not None:
+                for o in pair:
+                    pl.when(o != me)(functools.partial(ready, o))
+            slices = [compute(o) for o in pair]
+            for o, piece in zip(pair, slices):
+                buffer[o] = piece
+            for o in pair:
+                @pl.when(o != me)
+                def _():
+                    scatter(buffer, land, sems, o).start()
             return 0
 
-        lax.fori_loop(0, count - 1, one, 0)
+        lax.fori_loop(0, group // 2, one, 0)
+        land[me] = buffer[me]
 
     def owner_slice(pieces, norms):
         low = jnp.where(lanes < TILE // 2, norms[0], norms[1])
@@ -209,12 +222,8 @@
             norms.append(jnp.sum(feat, 1, keepdims=True))
         return owner_slice(pieces, norms)
 
-    def state_send(o):
-        p_send[o] = state_slice(o)
-        scatter(p_send, p_land, p_sems[0], o).start()
-
-    others(state_send)
-    p_land[me] = state_slice(me)
+    by_owner(state_slice, p_send, p_land, p_sems[0])
+    halo_copies[1].start()
 
     def query_features(h, _):
         feat, slope = feature(dot_nt(wq_ref[h], q_rows[h]) - SHIFT)
@@ -227,7 +236,7 @@
         by_head(c_raw, t * TILE, t * TILE, c_rows, TILE)
         load(3, t).wait()
         by_head(q_raw, t * TILE, t * TILE, q_rows, TILE)
-    lax.fori_loop(0, heads, query_features, 0)
+    lax.fori_loop(0, heads, query_features, 0, unroll=4)
 
     def local_terms(h, j, state, norm):
         cols = slice(j * TILE, (j + 1) * TILE)
@@ -274,18 +283,18 @@
         masked = jnp.concatenate([near, here], 0)
         weights = jnp.exp2(masked * scale2 - shift)
         rounded = weights.astype(BF16)
-        numer[h, cols, :] = dot_tn(rounded, v_window)
+        weight_rows[h, j] = rounded
         along = dot_nt(v_window, c_rows[h, cols, :])
         row_data[h, 0:1, cols] = jnp.exp2(-shift)
         row_data[h, 1:2, cols] = jnp.sum(weights, 0, keepdims=True)
-        row_data[h, 2:3, cols] = jnp.sum(rounded.astype(F32) * along, 0, keepdims=True)
+        row_data[h, 2:3, cols] = jnp.sum(weights * along, 0, keepdims=True)
 
     def sparse_tile(j):
         def one(h, _):
             sparse(h, j)
             return 0
 
-        lax.fori_loop(0, heads, one, 0)
+        lax.fori_loop(0, heads, one, 0, unroll=4)
 
     others(lambda s: arrival(p_send, p_land, p_sems[0], s).wait_recv())
     p_total[...] = sum(p_land[s] for s in range(1, group)) + p_land[0]
@@ -294,7 +303,7 @@
         def _():
             z_copy(p_total, p_far, p_sems[1], t).start()
 
-    lax.fori_loop(0, heads, local_states, 0)
+    lax.fori_loop(0, heads, local_states, 0, unroll=4)
     sparse_tile(1)
     sparse_tile(2)
 
@@ -328,7 +337,7 @@
         sparse(h, 0)
         return 0
 
-    lax.fori_loop(0, heads, halo_head, 0)
+    lax.fori_loop(0, heads, halo_head, 0, unroll=4)
 
     def d_slice(o):
         pieces, norms = [], []
@@ -347,7 +356,7 @@
             g = fq * share_of
             g_den = -share_of * ((row_data[h, 2:3, :] + decay * cu) * inverse)
             g_rows[h] = g
-            row_data[h, 5:6, :] = inverse
+            inverse_rows[h] = inverse
             gpre_q[h] = (
                 share_of * (u_local[h] + u_far) + g_den * (norm_local[h] + far_norm)
             ) * slope_q[h]
@@ -365,13 +374,10 @@
             norms.append(total_norm)
         return owner_slice(pieces, norms)
 
-    def d_send(o):
-        arrival(p_out, p_back, p_sems[2], o).wait_recv()
-        s_send[o] = d_slice(o)
-        scatter(s_send, s_land, s_sems[0], o).start()
-
-    others(d_send)
-    s_land[me] = d_slice(me)
+    by_owner(
+        d_slice, s_send, s_land, s_sems[0],
+        lambda o: arrival(p_out, p_back, p_sems[2], o).wait_recv(),
+    )
 
     def query_slice(o):
         pieces = []
@@ -380,12 +386,7 @@
             pieces.append(folded(dot_nn(stacked(gpre_q[h]), q_rows[h])))
         return jnp.concatenate(pieces, 0)
 
-    def query_send(o):
-        rq_send[o] = query_slice(o)
-        scatter(rq_send, rq_land, rq_sems[0], o).start()
-
-    others(query_send)
-    rq_land[me] = query_slice(me)
+    by_owner(query_slice, rq_send, rq_land, rq_sems[0])
 
     def key_local(h, _):
         parts = []
@@ -419,7 +420,7 @@
             cols = slice(j * TILE, (j + 1) * TILE)
             high, low = halves(far + state_local[h, j])
             g_high, g_low = halves(g_rows[h, :, cols])
-            first, rest = halves(row_data[h, 5:6, cols])
+            first, rest = halves(inverse_rows[h, :, cols])
             second, third = halves(rest)
             inverse = jnp.where(sub == 0, first, jnp.where(sub == 1, second, third))
             inverse = jnp.where(sub < 3, inverse, 0.0)
@@ -433,7 +434,9 @@
                 1,
             ).astype(BF16)
             both = dot_tn(left, right)
-            result = numer[h, cols, :] * both[:, TILE:] + both[:, :TILE]
+            window = slice(j * TILE, (j + 2) * TILE)
+            numer = dot_tn(weight_rows[h, j], v_rows[h, window, :])
+            result = numer * both[:, TILE:] + both[:, :TILE]
             o_rows[h, cols, :] = result.astype(BF16)
 
     def outputs_owner(o, _):
@@ -441,7 +444,7 @@
             outputs(o * own + i, o, i)
         return 0
 
-    lax.fori_loop(0, heads, key_local, 0)
+    lax.fori_loop(0, heads, key_local, 0, unroll=4)
 
     others(lambda s: arrival(s_send, s_land, s_sems[0], s).wait_recv())
     s_total[...] = sum(s_land[s] for s in range(1, group)) + s_land[0]
@@ -455,7 +458,7 @@
     others(lambda t: z_copy(rq_z, rq_zland, rq_sems[1], t).start(), nz, z)
     rq_zland[z] = rq_z[...]
 
-    lax.fori_loop(0, group, outputs_owner, 0)
+    lax.fori_loop(0, 4, outputs_owner, 0)
 
     acc[...] = jnp.zeros_like(acc)
     for t in range(1, nz):
@@ -476,14 +479,7 @@
     others(lambda t: x_copy(rq_x, rq_xland, rq_sems[2], t).start(), nx, x)
     rq_xland[x] = rq_x[...]
 
-    def by_position(b, _):
-        block = o_rows[:, pl.ds(b * BLOCK, BLOCK), :]
-        o_raw[pl.ds(b * BLOCK, BLOCK)] = jnp.swapaxes(block, 0, 1)
-        return 0
-
-    lax.fori_loop(0, tokens // BLOCK, by_position, 0, unroll=4)
-    store = pltpu.make_async_copy(o_raw, out_hbm, store_sem)
-    store.start()
+    lax.fori_loop(4, 6, outputs_owner, 0)
 
     def key_slice(o):
         pieces = []
@@ -496,18 +492,19 @@
             pieces.append(gk_local[h] + folded(dot_nn(stacked(grad), k_rows[h, own_rows, :])))
         return jnp.concatenate(pieces, 0)
 
-    def key_send(o):
-        arrival(s_out, s_back, s_sems[2], o).wait_recv()
-        rk_send[o] = key_slice(o)
-        scatter(rk_send, rk_land, rk_sems[0], o).start()
-
-    others(key_send)
-    rk_land[me] = key_slice(me)
+    by_owner(
+        key_slice, rk_send, rk_land, rk_sems[0],
+        lambda o: arrival(s_out, s_back, s_sems[2], o).wait_recv(),
+    )
 
     others(lambda t: x_arrival(rq_x, rq_xland, rq_sems[2], t).wait_recv(), nx, x)
     rq_sum[...] = sum(rq_xland[t] for t in range(1, nx)) + rq_xland[0]
     others(lambda s: share(rq_sum, gq_ref, rq_sems[3], s).start())
     gq_ref[me] = rq_sum[...]
+
+    lax.fori_loop(6, group, outputs_owner, 0)
+    store = pltpu.make_async_copy(o_rows, out_hbm, store_sem)
+    store.start()
 
     others(lambda s: arrival(rk_send, rk_land, rk_sems[0], s).wait_recv())
     rk_z[...] = sum(rk_land[s] for s in range(1, group)) + rk_land[0]
@@ -548,6 +545,17 @@
     store.wait()
 
 
+def finish(rows_ref, gq_ref, gk_ref, out_ref, gq_out, gk_out):
+    for b in range(out_ref.shape[0] // BLOCK):
+        rows = slice(b * BLOCK, (b + 1) * BLOCK)
+        out_ref[rows] = jnp.swapaxes(rows_ref[:, rows, :], 0, 1)
+
+    @pl.when(pl.program_id(0) == 0)
+    def _():
+        gq_out[...] = gq_ref[...]
+        gk_out[...] = gk_ref[...]
+
+
 def body(queries, keys, values, keep_count, query_map, key_map, cotangent):
     _, tokens, heads, width = queries.shape
     rank = query_map.shape[2]
@@ -579,14 +587,14 @@
     raw = (tokens, heads, width)
     lane_rows = (heads, rank, tokens)
     scratch = [
-        *[vmem(raw, BF16)] * 4, vmem((2, TILE, heads, width), BF16), vmem(raw, BF16),
+        *[vmem(raw, BF16)] * 4, vmem((2, TILE, heads, width), BF16),
         vmem((heads, tokens, width), BF16), vmem((heads, ext, width), BF16),
         vmem((heads, ext, width), BF16), vmem((heads, tokens, width), BF16),
-        vmem((heads, tokens, width), BF16), vmem((heads, tokens, width)),
+        vmem((heads, tokens, width), BF16), vmem((heads, tiles, 2 * TILE, TILE), BF16),
         vmem(lane_rows), vmem(lane_rows), vmem((heads, rank, ext)), vmem((heads, rank, ext)),
         vmem((heads, 8, ext)), vmem((tiles + 1, heads, 8, TILE), jnp.int32),
         vmem((heads, tiles, rank, width)), vmem(lane_rows), vmem(lane_rows),
-        vmem((heads, 8, tokens)), vmem(lane_rows), vmem(lane_rows),
+        vmem((heads, 8, tokens)), vmem((heads, 1, tokens)), vmem(lane_rows), vmem(lane_rows),
         vmem((heads, tiles, rank, width)), vmem((heads, tiles, rank, width)),
         vmem((heads, rank, width)),
         *scans(), *scans(), *sums(), *sums(), vmem(slab),
@@ -599,9 +607,9 @@
     anywhere = pl.BlockSpec(memory_space=pl.ANY)
     here = pl.BlockSpec(memory_space=pltpu.VMEM)
     grad = jax.ShapeDtypeStruct((group, *part), F32)
-    out, grad_q, grad_k = pl.pallas_call(
+    rows, grad_q, grad_k = pl.pallas_call(
         functools.partial(kernel, sizes),
-        out_shape=(jax.ShapeDtypeStruct(raw, BF16), grad, grad),
+        out_shape=(jax.ShapeDtypeStruct((heads, tokens, width), BF16), grad, grad),
         in_specs=[anywhere] * 4 + [here] * 3,
         out_specs=(anywhere, here, here),
         scratch_shapes=scratch,
@@ -614,6 +622,16 @@
         query_map.transpose(0, 2, 1), key_map.transpose(0, 2, 1),
     )
 
+    whole = pl.BlockSpec((group, *part), lambda t: (0, 0, 0))
+    out, grad_q, grad_k = pl.pallas_call(
+        finish,
+        grid=(tiles,),
+        out_shape=(jax.ShapeDtypeStruct(raw, BF16), grad, grad),
+        in_specs=[pl.BlockSpec((heads, TILE, width), lambda t: (0, t, 0)), whole, whole],
+        out_specs=(pl.BlockSpec((TILE, heads, width), lambda t: (t, 0, 0)), whole, whole),
+        name="finish",
+    )(rows, grad_q, grad_k)
+
     def map_grad(g):
         return g.reshape(heads, rank, width).transpose(0, 2, 1)
 

time: 105 us -> 75.5 us (0.72)
  Pallas kernels: 99.8 us -> 74.6 us
  local copies, waits for them, and re-layouts: 4.57 us -> 0 us
    pallas_call x1, Pallas kernels: 99.8 us -> 70.5 us  [body(): pl.pallas_call(functools.partial(kernel, sizes), out_shape=(jax.ShapeDtyp...]
    unnamed x7 -> x0, local copies, waits for them, and re-layouts: 4.57 us -> none
    pallas_call x0 -> x1, Pallas kernels: none -> 4.1 us  [body(): pl.pallas_call(finish, grid=(tiles,), out_shape=(jax.ShapeDtypeStruct(raw...]
where the time goes in v1:
time: 75.5 us; the launch traced here: 75.3 us
  Pallas kernels  74.6 us (99%)
    pallas_call x1, Pallas kernels, body(): pl.pallas_call(functools.partial(kernel, sizes), out_shape=(jax.ShapeDtyp...  70.5 us
    pallas_call x1, Pallas kernels, body(): pl.pallas_call(finish, grid=(tiles,), out_shape=(jax.ShapeDtypeStruct(raw...  4.1 us

profile of v1, /device:TPU:1, one launch (start us, length us, event | category | flops | bytes accessed | tf_op | source)
XLA Modules:
  0.0 75.3 jit_solution(9499642337898633163)
XLA Ops:
  0.6 70.5 %less_step.1 = (bf16[16,512,128]{2,1,0:T(8,128)(2,1)}, f32[8,16,128]{2,1,0:T(8,128)}, f32[8,16,128]{2,1,0:T(8,128)}) custom-call(bf16[512,16,128]{2,1,0:T(8,128)(2,1)} %bitcast.14, bf16[512,16,128]{2,1,0:T(8,128)(2,1)} %bitcast.15, bf16[512,16,128]{2,1,0:T(8,128)(2,1)} %bitcast.16, bf16[512,16,128]{2,1,0:T(8,128)(2,1)} %bitcast.17, s32[16,256]{1,0:T(8,128)} %bitcast.20, ...), custom_call_target="tpu_custom_call" | custom-call | tf_op jit(solution)/shard_map/less_step/pallas_call | solution.py:610
  71.2 4.1 %finish.1 = (bf16[512,16,128]{2,1,0:T(8,128)(2,1)}, f32[8,16,128]{2,1,0:T(8,128)}, f32[8,16,128]{2,1,0:T(8,128)}) custom-call(bf16[16,512,128]{2,1,0:T(8,128)(2,1)} %get-tuple-element.9.rows_ref, f32[8,16,128]{2,1,0:T(8,128)} %get-tuple-element.10.gq_ref, f32[8,16,128]{2,1,0:T(8,128)} %get-tuple-element.11.gk_ref), custom_call_target="tpu_custom_call" | custom-call | tf_op jit(solution)/shard_map/finish/pallas_call | solution.py:626

commit v2 on v1

--- a/solution.py
+++ b/solution.py
@@ -16,6 +16,7 @@
 SEQ = (Z_AXIS, Y_AXIS, C_AXIS)
 F32, BF16 = jnp.float32, jnp.bfloat16
 BLOCK = 16
+HALO_PIECES = ((0, 0, 64), (0, 64, 64), (1, 0, 128))
 
 
 def dot_nn(a, b):
@@ -63,8 +64,9 @@
 
 def kernel(
     sizes,
-    q_hbm, k_hbm, v_hbm, c_hbm, count_ref, wq_ref, wk_ref,
-    out_hbm, gq_ref, gk_ref,
+    q_hbm, k_hbm, v_hbm, c_hbm, count_hbm, wq_hbm, wk_hbm,
+    out_hbm, gq_hbm, gk_hbm,
+    count_ref, wq_ref, wk_ref, o_raw,
     q_raw, k_raw, v_raw, c_raw, halo_raw,
     q_rows, k_rows, v_rows, c_rows, o_rows, weight_rows,
     feat_q, slope_q, feat_k, slope_k, kept_lane, count_lane,
@@ -117,9 +119,18 @@
         rows = pl.ds(t * TILE, TILE)
         return pltpu.make_async_copy(sources[a].at[rows], raws[a].at[rows], load_sem.at[a * tiles + t])
 
+    small = [
+        pltpu.make_async_copy(source, target, load_sem.at[4 * tiles + n])
+        for n, (source, target) in enumerate(
+            ((wk_hbm, wk_ref), (count_hbm, count_ref), (wq_hbm, wq_ref))
+        )
+    ]
     for a in range(4):
         for t in range(tiles):
             load(a, t).start()
+        if a == 0:
+            for copy in small:
+                copy.start()
 
     def by_head(raw, rows, first, target, count):
         def step(b, _):
@@ -133,16 +144,18 @@
         load(0, t).wait()
         by_head(k_raw, t * TILE, (t + 1) * TILE, k_rows, TILE)
     pl.semaphore_wait(barrier, 2 + group - 1 + nz - 1 + nx - 1)
-    halo_from = pl.ds(tokens - TILE, TILE)
-    halo_copies = [
-        remote(k_hbm.at[halo_from], halo_raw.at[0], halo_sems.at[0], halo_sems.at[2], after),
-        remote(v_hbm.at[halo_from], halo_raw.at[1], halo_sems.at[1], halo_sems.at[3], after),
-    ]
+    halo_copies = []
+    for n, (a, first, count) in enumerate(HALO_PIECES):
+        source = (k_hbm, v_hbm)[a].at[pl.ds(tokens - TILE + first, count)]
+        target = halo_raw.at[a, pl.ds(first, count)]
+        halo_copies.append(remote(source, target, halo_sems.at[0, n], halo_sems.at[1, n], after))
     halo_copies[0].start()
     for t in range(tiles):
         load(1, t).wait()
         by_head(v_raw, t * TILE, (t + 1) * TILE, v_rows, TILE)
 
+    for copy in small:
+        copy.wait()
     counts = count_ref[...]
     which = lax.broadcasted_iota(jnp.int32, counts.shape, 1)
     lane16 = lax.broadcasted_iota(jnp.int32, (heads, TILE), 1)
@@ -223,7 +236,8 @@
         return owner_slice(pieces, norms)
 
     by_owner(state_slice, p_send, p_land, p_sems[0])
-    halo_copies[1].start()
+    for copy in halo_copies[1:]:
+        copy.start()
 
     def query_features(h, _):
         feat, slope = feature(dot_nt(wq_ref[h], q_rows[h]) - SHIFT)
@@ -249,21 +263,21 @@
         row_data[h, 4:5, cols] = jnp.sum(fq * u, 0, keepdims=True)
 
     def local_states(h, _):
-        full, full_norm, out, out_norm = [], [], [], []
-        for i in range(tiles - 1):
-            cols = slice((i + 1) * TILE, (i + 2) * TILE)
-            feat = feat_k[h, :, cols]
-            gone = feat * (1.0 - kept_lane[h, :, cols])
-            both = jnp.concatenate([*halves(feat), *halves(gone)], 0).astype(BF16)
-            result = dot_nn(both, v_rows[h, cols, :])
-            full.append(folded(result[:16]))
-            out.append(folded(result[16:]))
-            full_norm.append(jnp.sum(feat, 1, keepdims=True))
-            out_norm.append(jnp.sum(gone, 1, keepdims=True))
+        span = slice(TILE, tiles * TILE)
+        feat = feat_k[h, :, span]
+        gone = feat * (1.0 - kept_lane[h, :, span])
+        lines, norms = [], []
         for j in range(1, tiles):
-            local_terms(
-                h, j, sum(full[: j - 1], out[j - 1]), sum(full_norm[: j - 1], out_norm[j - 1])
-            )
+            cut = (j - 1) * TILE
+            pieces = [feat[:, :cut]] * (cut > 0) + [gone[:, cut : cut + TILE]]
+            pieces += [jnp.zeros((8, (tiles - 1 - j) * TILE), F32)] * (j < tiles - 1)
+            line = jnp.concatenate(pieces, 1)
+            lines += halves(line)
+            blocks = [line[:, i * TILE : (i + 1) * TILE] for i in range(j)]
+            norms.append(jnp.sum(sum(blocks[1:], blocks[0]), 1, keepdims=True))
+        result = dot_nn(jnp.concatenate(lines, 0).astype(BF16), v_rows[h, span, :])
+        for j in range(1, tiles):
+            local_terms(h, j, folded(result[(j - 1) * 16 : j * 16]), norms[j - 1])
         return 0
 
     scale2 = LOG2E / math.sqrt(width)
@@ -287,7 +301,7 @@
         along = dot_nt(v_window, c_rows[h, cols, :])
         row_data[h, 0:1, cols] = jnp.exp2(-shift)
         row_data[h, 1:2, cols] = jnp.sum(weights, 0, keepdims=True)
-        row_data[h, 2:3, cols] = jnp.sum(weights * along, 0, keepdims=True)
+        row_data[h, 2:3, cols] = jnp.sum(rounded.astype(F32) * along, 0, keepdims=True)
 
     def sparse_tile(j):
         def one(h, _):
@@ -499,25 +513,43 @@
 
     others(lambda t: x_arrival(rq_x, rq_xland, rq_sems[2], t).wait_recv(), nx, x)
     rq_sum[...] = sum(rq_xland[t] for t in range(1, nx)) + rq_xland[0]
-    others(lambda s: share(rq_sum, gq_ref, rq_sems[3], s).start())
-    gq_ref[me] = rq_sum[...]
+    others(lambda s: share(rq_sum, gq_hbm, rq_sems[3], s).start())
+    own_gq = pltpu.make_async_copy(rq_sum, gq_hbm.at[me], store_sem.at[tiles])
+    own_gq.start()
 
     lax.fori_loop(6, group, outputs_owner, 0)
-    store = pltpu.make_async_copy(o_rows, out_hbm, store_sem)
-    store.start()
+
+    def by_position(b, _):
+        block = o_rows[:, pl.ds(b * BLOCK, BLOCK), :]
+        o_raw[pl.ds(b * BLOCK, BLOCK)] = jnp.swapaxes(block, 0, 1)
+        return 0
+
+    stores = []
+
+    def store(t):
+        blocks = TILE // BLOCK
+        lax.fori_loop(t * blocks, (t + 1) * blocks, by_position, 0, unroll=4)
+        rows = pl.ds(t * TILE, TILE)
+        stores.append(pltpu.make_async_copy(o_raw.at[rows], out_hbm.at[rows], store_sem.at[t]))
+        stores[-1].start()
+
+    store(0)
 
     others(lambda s: arrival(rk_send, rk_land, rk_sems[0], s).wait_recv())
     rk_z[...] = sum(rk_land[s] for s in range(1, group)) + rk_land[0]
     others(lambda t: z_copy(rk_z, rk_zland, rk_sems[1], t).start(), nz, z)
     rk_zland[z] = rk_z[...]
+    for t in range(1, tiles):
+        store(t)
     others(lambda t: z_arrival(rk_z, rk_zland, rk_sems[1], t).wait_recv(), nz, z)
     rk_x[...] = sum(rk_zland[t] for t in range(1, nz)) + rk_zland[0]
     others(lambda t: x_copy(rk_x, rk_xland, rk_sems[2], t).start(), nx, x)
     rk_xland[x] = rk_x[...]
     others(lambda t: x_arrival(rk_x, rk_xland, rk_sems[2], t).wait_recv(), nx, x)
     rk_sum[...] = sum(rk_xland[t] for t in range(1, nx)) + rk_xland[0]
-    others(lambda s: share(rk_sum, gk_ref, rk_sems[3], s).start())
-    gk_ref[me] = rk_sum[...]
+    others(lambda s: share(rk_sum, gk_hbm, rk_sems[3], s).start())
+    own_gk = pltpu.make_async_copy(rk_sum, gk_hbm.at[me], store_sem.at[tiles + 1])
+    own_gk.start()
 
     for copy in halo_copies:
         copy.wait_send()
@@ -534,26 +566,33 @@
         def _():
             z_copy(s_total, s_far, s_sems[1], t).wait_send()
     for send, land, zs, zland, xs, xland, total, grad, sems in (
-        (rq_send, rq_land, rq_z, rq_zland, rq_x, rq_xland, rq_sum, gq_ref, rq_sems),
-        (rk_send, rk_land, rk_z, rk_zland, rk_x, rk_xland, rk_sum, gk_ref, rk_sems),
+        (rq_send, rq_land, rq_z, rq_zland, rq_x, rq_xland, rq_sum, gq_hbm, rq_sems),
+        (rk_send, rk_land, rk_z, rk_zland, rk_x, rk_xland, rk_sum, gk_hbm, rk_sems),
     ):
         others(lambda s: scatter(send, land, sems[0], s).wait_send())
         others(lambda t: z_copy(zs, zland, sems[1], t).wait_send(), nz, z)
         others(lambda t: x_copy(xs, xland, sems[2], t).wait_send(), nx, x)
         others(lambda s: share(total, grad, sems[3], s).wait_send())
         others(lambda s: share_arrival(total, grad, sems[3], s).wait_recv())
-    store.wait()
-
-
-def finish(rows_ref, gq_ref, gk_ref, out_ref, gq_out, gk_out):
-    for b in range(out_ref.shape[0] // BLOCK):
-        rows = slice(b * BLOCK, (b + 1) * BLOCK)
-        out_ref[rows] = jnp.swapaxes(rows_ref[:, rows, :], 0, 1)
-
-    @pl.when(pl.program_id(0) == 0)
-    def _():
-        gq_out[...] = gq_ref[...]
-        gk_out[...] = gk_ref[...]
+    for copy in (*stores, own_gq, own_gk):
+        copy.wait()
+
+
+def finish(rows_hbm, gq_hbm, gk_hbm, out_hbm, gq_out, gk_out, rows, gq, gk, sems):
+    parts = rows.shape[0] // TILE
+    moves = [(gq_hbm, gq, gq_out), (gk_hbm, gk, gk_out)]
+    for t in range(parts):
+        span = pl.ds(t * TILE, TILE)
+        moves.append((rows_hbm.at[span], rows.at[span], out_hbm.at[span]))
+    ins = [pltpu.make_async_copy(a, b, sems.at[0, n]) for n, (a, b, _) in enumerate(moves)]
+    outs = [pltpu.make_async_copy(b, c, sems.at[1, n]) for n, (_, b, c) in enumerate(moves)]
+    for copy in ins:
+        copy.start()
+    for arrived, copy in zip(ins, outs):
+        arrived.wait()
+        copy.start()
+    for copy in outs:
+        copy.wait()
 
 
 def body(queries, keys, values, keep_count, query_map, key_map, cotangent):
@@ -586,7 +625,9 @@
 
     raw = (tokens, heads, width)
     lane_rows = (heads, rank, tokens)
+    small = [vmem((heads, nz * group * tiles), jnp.int32), *[vmem((heads, rank, width), BF16)] * 2]
     scratch = [
+        *small, vmem(raw, BF16),
         *[vmem(raw, BF16)] * 4, vmem((2, TILE, heads, width), BF16),
         vmem((heads, tokens, width), BF16), vmem((heads, ext, width), BF16),
         vmem((heads, ext, width), BF16), vmem((heads, tokens, width), BF16),
@@ -598,20 +639,19 @@
         vmem((heads, tiles, rank, width)), vmem((heads, tiles, rank, width)),
         vmem((heads, rank, width)),
         *scans(), *scans(), *sums(), *sums(), vmem(slab),
-        dma((4 * tiles,)), dma, dma((4,)),
+        dma((4 * tiles + 3,)), dma((tiles + 2,)), dma((2, len(HALO_PIECES))),
         [dma((2 * group,)), dma((2 * nz,)), dma((2 * group,))],
         [dma((2 * group,)), dma((2 * nz,)), dma((2 * group,))],
         [dma((2 * group,)), dma((2 * nz,)), dma((2 * nx,)), dma((2 * group,))],
         [dma((2 * group,)), dma((2 * nz,)), dma((2 * nx,)), dma((2 * group,))],
     ]
     anywhere = pl.BlockSpec(memory_space=pl.ANY)
-    here = pl.BlockSpec(memory_space=pltpu.VMEM)
     grad = jax.ShapeDtypeStruct((group, *part), F32)
     rows, grad_q, grad_k = pl.pallas_call(
         functools.partial(kernel, sizes),
-        out_shape=(jax.ShapeDtypeStruct((heads, tokens, width), BF16), grad, grad),
-        in_specs=[anywhere] * 4 + [here] * 3,
-        out_specs=(anywhere, here, here),
+        out_shape=(jax.ShapeDtypeStruct(raw, BF16), grad, grad),
+        in_specs=[anywhere] * 7,
+        out_specs=(anywhere,) * 3,
         scratch_shapes=scratch,
         compiler_params=pltpu.CompilerParams(
             collective_id=0, has_side_effects=True, vmem_limit_bytes=60 * 2**20
@@ -622,13 +662,14 @@
         query_map.transpose(0, 2, 1), key_map.transpose(0, 2, 1),
     )
 
-    whole = pl.BlockSpec((group, *part), lambda t: (0, 0, 0))
     out, grad_q, grad_k = pl.pallas_call(
         finish,
-        grid=(tiles,),
         out_shape=(jax.ShapeDtypeStruct(raw, BF16), grad, grad),
-        in_specs=[pl.BlockSpec((heads, TILE, width), lambda t: (0, t, 0)), whole, whole],
-        out_specs=(pl.BlockSpec((TILE, heads, width), lambda t: (t, 0, 0)), whole, whole),
+        in_specs=[anywhere] * 3,
+        out_specs=(anywhere,) * 3,
+        scratch_shapes=[
+            vmem(raw, BF16), vmem((group, *part)), vmem((group, *part)), dma((2, tiles + 2)),
+        ],
         name="finish",
     )(rows, grad_q, grad_k)
 

time: 75.5 us -> 72.5 us (0.960)
  Pallas kernels: 74.6 us -> 71.7 us
    pallas_call x1, Pallas kernels: 4.1 us -> 2.54 us  [body(): pl.pallas_call(finish, out_shape=(jax.ShapeDtypeStruct(raw, BF16), grad,...]
    pallas_call x1, Pallas kernels: 70.5 us -> 69.2 us  [body(): pl.pallas_call(functools.partial(kernel, sizes), out_shape=(jax.ShapeDtyp...]
where the time goes in v2:
time: 72.5 us; the launch traced here: 72.4 us
  Pallas kernels  71.7 us (99%)
    pallas_call x1, Pallas kernels, body(): pl.pallas_call(functools.partial(kernel, sizes), out_shape=(jax.ShapeDtyp...  69.2 us
    pallas_call x1, Pallas kernels, body(): pl.pallas_call(finish, out_shape=(jax.ShapeDtypeStruct(raw, BF16), grad,...  2.54 us

profile of v2, /device:TPU:1, one launch (start us, length us, event | category | flops | bytes accessed | tf_op | source)
XLA Modules:
  0.0 72.4 jit_solution(17179609083699775261)
XLA Ops:
  0.6 69.2 %less_step.1 = (bf16[512,16,128]{2,1,0:T(8,128)(2,1)}, f32[8,16,128]{2,1,0:T(8,128)}, f32[8,16,128]{2,1,0:T(8,128)}) custom-call(bf16[512,16,128]{2,1,0:T(8,128)(2,1)} %bitcast.14, bf16[512,16,128]{2,1,0:T(8,128)(2,1)} %bitcast.15, bf16[512,16,128]{2,1,0:T(8,128)(2,1)} %bitcast.16, bf16[512,16,128]{2,1,0:T(8,128)(2,1)} %bitcast.17, s32[16,256]{1,0:T(8,128)} %bitcast.20, ...), custom_call_target="tpu_custom_call" | custom-call | tf_op jit(solution)/shard_map/less_step/pallas_call | solution.py:650
  69.8 2.5 %finish.1 = (bf16[512,16,128]{2,1,0:T(8,128)(2,1)}, f32[8,16,128]{2,1,0:T(8,128)}, f32[8,16,128]{2,1,0:T(8,128)}) custom-call(bf16[512,16,128]{2,1,0:T(8,128)(2,1)} %get-tuple-element.9.rows_hbm, f32[8,16,128]{2,1,0:T(8,128)} %get-tuple-element.10.gq_hbm, f32[8,16,128]{2,1,0:T(8,128)} %get-tuple-element.11.gk_hbm), custom_call_target="tpu_custom_call" | custom-call | tf_op jit(solution)/shard_map/finish/pallas_call | solution.py:665

commit v3 on v2

--- a/solution.py
+++ b/solution.py
@@ -70,7 +70,7 @@
     q_raw, k_raw, v_raw, c_raw, halo_raw,
     q_rows, k_rows, v_rows, c_rows, o_rows, weight_rows,
     feat_q, slope_q, feat_k, slope_k, kept_lane, count_lane,
-    state_local, norm_local, u_local, row_data, inverse_rows, g_rows, gpre_q, d_state, d_norm, gk_local,
+    state_local, norm_local, u_local, row_data, inverse_rows, g_rows, gpre_q, d_state, d_norm, gk_local, far_rows,
     p_send, p_land, p_total, p_far, p_out, p_back,
     s_send, s_land, s_total, s_far, s_out, s_back,
     rq_send, rq_land, rq_z, rq_zland, rq_x, rq_xland, rq_sum,
@@ -150,11 +150,20 @@
         target = halo_raw.at[a, pl.ds(first, count)]
         halo_copies.append(remote(source, target, halo_sems.at[0, n], halo_sems.at[1, n], after))
     halo_copies[0].start()
+    small[0].wait()
+
+    def key_features(h, _):
+        feat, slope = feature(dot_nt(wk_ref[h], k_rows[h, pl.ds(TILE, tokens), :]) - SHIFT)
+        feat_k[h, :, TILE:] = feat
+        slope_k[h, :, TILE:] = slope
+        return 0
+
+    lax.fori_loop(0, heads, key_features, 0, unroll=4)
     for t in range(tiles):
         load(1, t).wait()
         by_head(v_raw, t * TILE, (t + 1) * TILE, v_rows, TILE)
 
-    for copy in small:
+    for copy in small[1:]:
         copy.wait()
     counts = count_ref[...]
     which = lax.broadcasted_iota(jnp.int32, counts.shape, 1)
@@ -196,12 +205,16 @@
         for k in sorted(range(1, count), key=lambda k: -min(k, count - k)):
             step((here + k) % count)
 
-    def by_owner(compute, buffer, land, sems, ready=None):
+    def nearer(k, steps):
+        found = []
+        for n in range(steps):
+            n = k * steps + n
+            found += [(me + group // 2 - n) % group, (me + group // 2 + 1 + n) % group]
+        return found
+
+    def by_owner(compute, buffer, land, sems, steps=1):
         def one(k, _):
-            pair = [(me + group // 2 - k) % group, (me + group // 2 + 1 + k) % group]
-            if ready is not None:
-                for o in pair:
-                    pl.when(o != me)(functools.partial(ready, o))
+            pair = nearer(k, steps)
             slices = [compute(o) for o in pair]
             for o, piece in zip(pair, slices):
                 buffer[o] = piece
@@ -211,7 +224,7 @@
                     scatter(buffer, land, sems, o).start()
             return 0
 
-        lax.fori_loop(0, group // 2, one, 0)
+        lax.fori_loop(0, group // 2 // steps, one, 0)
         land[me] = buffer[me]
 
     def owner_slice(pieces, norms):
@@ -223,14 +236,31 @@
         return jnp.where(lanes < TILE // 2, *((tile, turned) if i == 0 else (turned, tile)))
 
     own_rows = pl.ds(TILE, tokens)
+
+    def each_head(step):
+        def one(h, _):
+            step(h)
+            return 0
+
+        lax.fori_loop(0, heads, one, 0, unroll=4)
+
+    def each_owner(step, ready):
+        def one(k, _):
+            pair = nearer(k, 1)
+            for o in pair:
+                pl.when(o != me)(functools.partial(ready, o))
+            for o in pair:
+                for i in range(own):
+                    step(o, i)
+            return 0
+
+        lax.fori_loop(0, group // 2, one, 0)
 
     def state_slice(o):
         pieces, norms = [], []
         for i in range(own):
             h = o * own + i
-            feat, slope = feature(dot_nt(wk_ref[h], k_rows[h, own_rows, :]) - SHIFT)
-            feat_k[h, :, TILE:] = feat
-            slope_k[h, :, TILE:] = slope
+            feat = feat_k[h, :, TILE:]
             pieces.append(folded(dot_nn(stacked(feat), v_rows[h, own_rows, :])))
             norms.append(jnp.sum(feat, 1, keepdims=True))
         return owner_slice(pieces, norms)
@@ -252,14 +282,16 @@
         by_head(q_raw, t * TILE, t * TILE, q_rows, TILE)
     lax.fori_loop(0, heads, query_features, 0, unroll=4)
 
-    def local_terms(h, j, state, norm):
+    def keep_state(h, j, state, norm):
+        state_local[h, j] = state
+        norm_local[h, :, j * TILE : (j + 1) * TILE] = jnp.broadcast_to(norm, (8, TILE))
+
+    def local_products(h, j):
         cols = slice(j * TILE, (j + 1) * TILE)
-        state_local[h, j] = state
-        norm_local[h, :, cols] = jnp.broadcast_to(norm, (8, TILE))
-        u = folded(dot_nt(stacked(state), c_rows[h, cols, :]))
+        u = folded(dot_nt(stacked(state_local[h, j]), c_rows[h, cols, :]))
         u_local[h, :, cols] = u
         fq = feat_q[h, :, cols]
-        row_data[h, 3:4, cols] = jnp.sum(fq * norm, 0, keepdims=True)
+        row_data[h, 3:4, cols] = jnp.sum(fq * norm_local[h, :, cols], 0, keepdims=True)
         row_data[h, 4:5, cols] = jnp.sum(fq * u, 0, keepdims=True)
 
     def local_states(h, _):
@@ -277,7 +309,7 @@
             norms.append(jnp.sum(sum(blocks[1:], blocks[0]), 1, keepdims=True))
         result = dot_nn(jnp.concatenate(lines, 0).astype(BF16), v_rows[h, span, :])
         for j in range(1, tiles):
-            local_terms(h, j, folded(result[(j - 1) * 16 : j * 16]), norms[j - 1])
+            keep_state(h, j, folded(result[(j - 1) * 16 : j * 16]), norms[j - 1])
         return 0
 
     scale2 = LOG2E / math.sqrt(width)
@@ -318,6 +350,7 @@
             z_copy(p_total, p_far, p_sems[1], t).start()
 
     lax.fori_loop(0, heads, local_states, 0, unroll=4)
+    each_head(lambda h: [local_products(h, j) for j in range(1, tiles)])
     sparse_tile(1)
     sparse_tile(2)
 
@@ -342,26 +375,29 @@
     by_head(halo_raw.at[0], 0, 0, k_rows, TILE)
     by_head(halo_raw.at[1], 0, 0, v_rows, TILE)
 
-    def halo_head(h, _):
+    def halo_features(h):
         feat, slope = feature(dot_nt(wk_ref[h], k_rows[h, :TILE, :]) - SHIFT)
         slope_k[h, :, :TILE] = slope
-        held = feat * kept_lane[h, :, :TILE]
+        feat_k[h, :, :TILE] = feat * kept_lane[h, :, :TILE]
+
+    def halo_state(h):
+        held = feat_k[h, :, :TILE]
         state = folded(dot_nn(stacked(held), v_rows[h, :TILE, :]))
-        local_terms(h, 0, -state, -jnp.sum(held, 1, keepdims=True))
-        sparse(h, 0)
-        return 0
-
-    lax.fori_loop(0, heads, halo_head, 0, unroll=4)
+        keep_state(h, 0, -state, -jnp.sum(held, 1, keepdims=True))
+
+    each_head(halo_features)
+    each_head(halo_state)
+    each_head(lambda h: local_products(h, 0))
+    sparse_tile(0)
 
     def d_slice(o):
         pieces, norms = [], []
         back = p_back[o]
         for i in range(own):
             h = o * own + i
-            far = back[i * 8 : (i + 1) * 8]
             far_norm = jnp.concatenate([norm_of(back[own * 8 :], i)] * tiles, 1)
             fq = feat_q[h]
-            u_far = folded(dot_nt(stacked(far), c_rows[h]))
+            u_far = far_rows[h]
             decay = row_data[h, 0:1, :]
             kd = row_data[h, 3:4, :] + jnp.sum(fq * far_norm, 0, keepdims=True)
             cu = row_data[h, 4:5, :] + jnp.sum(fq * u_far, 0, keepdims=True)
@@ -388,10 +424,12 @@
             norms.append(total_norm)
         return owner_slice(pieces, norms)
 
-    by_owner(
-        d_slice, s_send, s_land, s_sems[0],
-        lambda o: arrival(p_out, p_back, p_sems[2], o).wait_recv(),
-    )
+    def far_products(o, i):
+        far = p_back[o, i * 8 : (i + 1) * 8]
+        far_rows[o * own + i] = folded(dot_nt(stacked(far), c_rows[o * own + i]))
+
+    each_owner(far_products, lambda o: arrival(p_out, p_back, p_sems[2], o).wait_recv())
+    by_owner(d_slice, s_send, s_land, s_sems[0], 2)
 
     def query_slice(o):
         pieces = []
@@ -402,7 +440,7 @@
 
     by_owner(query_slice, rq_send, rq_land, rq_sems[0])
 
-    def key_local(h, _):
+    def key_local(h):
         parts = []
         for e in range(tiles):
             cols = slice(e * TILE, (e + 1) * TILE)
@@ -422,8 +460,10 @@
                 else:
                     grad = (1.0 - kept) * (folded(dot_nt(stacked(near), v_tile)) + near_norm)
             parts.append(grad * slope_k[h, :, cols])
-        gk_local[h] = folded(dot_nn(stacked(jnp.concatenate(parts, 1)), k_rows[h, :tokens, :]))
-        return 0
+        far_rows[h] = jnp.concatenate(parts, 1)
+
+    def key_gradient(h):
+        gk_local[h] = folded(dot_nn(stacked(far_rows[h]), k_rows[h, :tokens, :]))
 
     sub = lax.broadcasted_iota(jnp.int32, (8, TILE), 0)
 
@@ -458,7 +498,8 @@
             outputs(o * own + i, o, i)
         return 0
 
-    lax.fori_loop(0, heads, key_local, 0, unroll=4)
+    each_head(key_local)
+    each_head(key_gradient)
 
     others(lambda s: arrival(s_send, s_land, s_sems[0], s).wait_recv())
     s_total[...] = sum(s_land[s] for s in range(1, group)) + s_land[0]
@@ -495,21 +536,22 @@
 
     lax.fori_loop(4, 6, outputs_owner, 0)
 
+    def key_products(o, i):
+        h = o * own + i
+        back = s_back[o]
+        far_norm = jnp.concatenate([norm_of(back[own * 8 :], i)] * tiles, 1)
+        grad = folded(dot_nt(stacked(back[i * 8 : (i + 1) * 8]), v_rows[h, own_rows, :]))
+        far_rows[h] = (grad + far_norm) * slope_k[h, :, TILE:]
+
     def key_slice(o):
         pieces = []
-        back = s_back[o]
         for i in range(own):
             h = o * own + i
-            far_norm = jnp.concatenate([norm_of(back[own * 8 :], i)] * tiles, 1)
-            grad = folded(dot_nt(stacked(back[i * 8 : (i + 1) * 8]), v_rows[h, own_rows, :]))
-            grad = (grad + far_norm) * slope_k[h, :, TILE:]
-            pieces.append(gk_local[h] + folded(dot_nn(stacked(grad), k_rows[h, own_rows, :])))
+            pieces.append(gk_local[h] + folded(dot_nn(stacked(far_rows[h]), k_rows[h, own_rows, :])))
         return jnp.concatenate(pieces, 0)
 
-    by_owner(
-        key_slice, rk_send, rk_land, rk_sems[0],
-        lambda o: arrival(s_out, s_back, s_sems[2], o).wait_recv(),
-    )
+    each_owner(key_products, lambda o: arrival(s_out, s_back, s_sems[2], o).wait_recv())
+    by_owner(key_slice, rk_send, rk_land, rk_sems[0])
 
     others(lambda t: x_arrival(rq_x, rq_xland, rq_sems[2], t).wait_recv(), nx, x)
     rq_sum[...] = sum(rq_xland[t] for t in range(1, nx)) + rq_xland[0]
@@ -637,7 +679,7 @@
         vmem((heads, tiles, rank, width)), vmem(lane_rows), vmem(lane_rows),
         vmem((heads, 8, tokens)), vmem((heads, 1, tokens)), vmem(lane_rows), vmem(lane_rows),
         vmem((heads, tiles, rank, width)), vmem((heads, tiles, rank, width)),
-        vmem((heads, rank, width)),
+        vmem((heads, rank, width)), vmem(lane_rows),
         *scans(), *scans(), *sums(), *sums(), vmem(slab),
         dma((4 * tiles + 3,)), dma((tiles + 2,)), dma((2, len(HALO_PIECES))),
         [dma((2 * group,)), dma((2 * nz,)), dma((2 * group,))],

time: 72.5 us -> 72.4 us (level)
  no operation moved by 1% of the time
where the time goes in v3:
time: 72.4 us; the launch traced here: 72.3 us
  Pallas kernels  71.6 us (99%)
    pallas_call x1, Pallas kernels, body(): pl.pallas_call(functools.partial(kernel, sizes), out_shape=(jax.ShapeDtyp...  69.1 us
    pallas_call x1, Pallas kernels, body(): pl.pallas_call(finish, out_shape=(jax.ShapeDtypeStruct(raw, BF16), grad,...  2.54 us

profile of v3, /device:TPU:1, one launch (start us, length us, event | category | flops | bytes accessed | tf_op | source)
XLA Modules:
  0.0 72.3 jit_solution(5962096112546507499)
XLA Ops:
  0.6 69.1 %less_step.1 = (bf16[512,16,128]{2,1,0:T(8,128)(2,1)}, f32[8,16,128]{2,1,0:T(8,128)}, f32[8,16,128]{2,1,0:T(8,128)}) custom-call(bf16[512,16,128]{2,1,0:T(8,128)(2,1)} %bitcast.14, bf16[512,16,128]{2,1,0:T(8,128)(2,1)} %bitcast.15, bf16[512,16,128]{2,1,0:T(8,128)(2,1)} %bitcast.16, bf16[512,16,128]{2,1,0:T(8,128)(2,1)} %bitcast.17, s32[16,256]{1,0:T(8,128)} %bitcast.20, ...), custom_call_target="tpu_custom_call" | custom-call | tf_op jit(solution)/shard_map/less_step/pallas_call | solution.py:692
  69.7 2.5 %finish.1 = (bf16[512,16,128]{2,1,0:T(8,128)(2,1)}, f32[8,16,128]{2,1,0:T(8,128)}, f32[8,16,128]{2,1,0:T(8,128)}) custom-call(bf16[512,16,128]{2,1,0:T(8,128)(2,1)} %get-tuple-element.9.rows_hbm, f32[8,16,128]{2,1,0:T(8,128)} %get-tuple-element.10.gq_hbm, f32[8,16,128]{2,1,0:T(8,128)} %get-tuple-element.11.gk_hbm), custom_call_target="tpu_custom_call" | custom-call | tf_op jit(solution)/shard_map/finish/pallas_call | solution.py:707

commit v4 on v3

--- a/solution.py
+++ b/solution.py
@@ -158,7 +158,7 @@
         slope_k[h, :, TILE:] = slope
         return 0
 
-    lax.fori_loop(0, heads, key_features, 0, unroll=4)
+    lax.fori_loop(0, heads, key_features, 0, unroll=8)
     for t in range(tiles):
         load(1, t).wait()
         by_head(v_raw, t * TILE, (t + 1) * TILE, v_rows, TILE)
@@ -237,16 +237,16 @@
 
     own_rows = pl.ds(TILE, tokens)
 
-    def each_head(step):
+    def each_head(step, unroll=4):
         def one(h, _):
             step(h)
             return 0
 
-        lax.fori_loop(0, heads, one, 0, unroll=4)
+        lax.fori_loop(0, heads, one, 0, unroll=unroll)
 
     def each_owner(step, ready):
         def one(k, _):
-            pair = nearer(k, 1)
+            pair = nearer(k, 2)
             for o in pair:
                 pl.when(o != me)(functools.partial(ready, o))
             for o in pair:
@@ -254,7 +254,7 @@
                     step(o, i)
             return 0
 
-        lax.fori_loop(0, group // 2, one, 0)
+        lax.fori_loop(0, group // 4, one, 0)
 
     def state_slice(o):
         pieces, norms = [], []
@@ -265,7 +265,7 @@
             norms.append(jnp.sum(feat, 1, keepdims=True))
         return owner_slice(pieces, norms)
 
-    by_owner(state_slice, p_send, p_land, p_sems[0])
+    by_owner(state_slice, p_send, p_land, p_sems[0], 2)
     for copy in halo_copies[1:]:
         copy.start()
 
@@ -280,7 +280,7 @@
         by_head(c_raw, t * TILE, t * TILE, c_rows, TILE)
         load(3, t).wait()
         by_head(q_raw, t * TILE, t * TILE, q_rows, TILE)
-    lax.fori_loop(0, heads, query_features, 0, unroll=4)
+    lax.fori_loop(0, heads, query_features, 0, unroll=8)
 
     def keep_state(h, j, state, norm):
         state_local[h, j] = state
@@ -316,24 +316,28 @@
     key_at = lax.broadcasted_iota(jnp.int32, (TILE, TILE), 0)
     causal = key_at <= lax.broadcasted_iota(jnp.int32, (TILE, TILE), 1)
 
-    def sparse(h, j):
+    def weigh(h, j):
         cols = slice(j * TILE, (j + 1) * TILE)
-        window = slice(j * TILE, (j + 2) * TILE)
-        v_window = v_rows[h, window, :]
-        scores = dot_nt(k_rows[h, window, :], q_rows[h, cols, :])
+        scores = dot_nt(k_rows[h, j * TILE : (j + 2) * TILE, :], q_rows[h, cols, :])
         live = key_at < count_lane[j, h, 0:1, :]
         near = jnp.where(live, scores[:TILE], -1e30)
         here = jnp.where(causal, scores[TILE:], -1e30)
         top = jnp.maximum(jnp.max(near, 0, keepdims=True), jnp.max(here, 0, keepdims=True))
         shift = top * scale2
-        masked = jnp.concatenate([near, here], 0)
-        weights = jnp.exp2(masked * scale2 - shift)
+        weights = jnp.exp2(jnp.concatenate([near, here], 0) * scale2 - shift)
         rounded = weights.astype(BF16)
         weight_rows[h, j] = rounded
-        along = dot_nt(v_window, c_rows[h, cols, :])
         row_data[h, 0:1, cols] = jnp.exp2(-shift)
         row_data[h, 1:2, cols] = jnp.sum(weights, 0, keepdims=True)
-        row_data[h, 2:3, cols] = jnp.sum(rounded.astype(F32) * along, 0, keepdims=True)
+        return rounded
+
+    def along(h, j, rounded):
+        cols = slice(j * TILE, (j + 1) * TILE)
+        product = dot_nt(v_rows[h, j * TILE : (j + 2) * TILE, :], c_rows[h, cols, :])
+        row_data[h, 2:3, cols] = jnp.sum(rounded.astype(F32) * product, 0, keepdims=True)
+
+    def sparse(h, j):
+        along(h, j, weigh(h, j))
 
     def sparse_tile(j):
         def one(h, _):
@@ -349,8 +353,8 @@
         def _():
             z_copy(p_total, p_far, p_sems[1], t).start()
 
-    lax.fori_loop(0, heads, local_states, 0, unroll=4)
-    each_head(lambda h: [local_products(h, j) for j in range(1, tiles)])
+    lax.fori_loop(0, heads, local_states, 0, unroll=8)
+    each_head(lambda h: [local_products(h, j) for j in range(1, tiles)], 8)
     sparse_tile(1)
     sparse_tile(2)
 
@@ -370,11 +374,6 @@
 
     sparse_tile(3)
 
-    for copy in halo_copies:
-        copy.wait_recv()
-    by_head(halo_raw.at[0], 0, 0, k_rows, TILE)
-    by_head(halo_raw.at[1], 0, 0, v_rows, TILE)
-
     def halo_features(h):
         feat, slope = feature(dot_nt(wk_ref[h], k_rows[h, :TILE, :]) - SHIFT)
         slope_k[h, :, :TILE] = slope
@@ -385,10 +384,22 @@
         state = folded(dot_nn(stacked(held), v_rows[h, :TILE, :]))
         keep_state(h, 0, -state, -jnp.sum(held, 1, keepdims=True))
 
-    each_head(halo_features)
-    each_head(halo_state)
-    each_head(lambda h: local_products(h, 0))
-    sparse_tile(0)
+    def halo_along(h):
+        local_products(h, 0)
+        along(h, 0, weight_rows[h, 0])
+
+    for copy, (a, _, _) in zip(halo_copies, HALO_PIECES):
+        if a == 0:
+            copy.wait_recv()
+    by_head(halo_raw.at[0], 0, 0, k_rows, TILE)
+    each_head(halo_features, 8)
+    each_head(lambda h: weigh(h, 0))
+    for copy, (a, _, _) in zip(halo_copies, HALO_PIECES):
+        if a == 1:
+            copy.wait_recv()
+    by_head(halo_raw.at[1], 0, 0, v_rows, TILE)
+    each_head(halo_state, 16)
+    each_head(halo_along, 8)
 
     def d_slice(o):
         pieces, norms = [], []
@@ -438,7 +449,7 @@
             pieces.append(folded(dot_nn(stacked(gpre_q[h]), q_rows[h])))
         return jnp.concatenate(pieces, 0)
 
-    by_owner(query_slice, rq_send, rq_land, rq_sems[0])
+    by_owner(query_slice, rq_send, rq_land, rq_sems[0], 2)
 
     def key_local(h):
         parts = []
@@ -498,8 +509,8 @@
             outputs(o * own + i, o, i)
         return 0
 
-    each_head(key_local)
-    each_head(key_gradient)
+    each_head(key_local, 8)
+    each_head(key_gradient, 8)
 
     others(lambda s: arrival(s_send, s_land, s_sems[0], s).wait_recv())
     s_total[...] = sum(s_land[s] for s in range(1, group)) + s_land[0]
@@ -551,7 +562,7 @@
         return jnp.concatenate(pieces, 0)
 
     each_owner(key_products, lambda o: arrival(s_out, s_back, s_sems[2], o).wait_recv())
-    by_owner(key_slice, rk_send, rk_land, rk_sems[0])
+    by_owner(key_slice, rk_send, rk_land, rk_sems[0], 2)
 
     others(lambda t: x_arrival(rq_x, rq_xland, rq_sems[2], t).wait_recv(), nx, x)
     rq_sum[...] = sum(rq_xland[t] for t in range(1, nx)) + rq_xland[0]

time: 72.4 us -> 71 us (0.981)
  Pallas kernels: 71.6 us -> 70.3 us
    pallas_call x1, Pallas kernels: 69.1 us -> 67.7 us  [body(): pl.pallas_call(functools.partial(kernel, sizes), out_shape=(jax.ShapeDtyp...]
where the time goes in v4:
time: 71 us; the launch traced here: 70.9 us
  Pallas kernels  70.3 us (99%)
    pallas_call x1, Pallas kernels, body(): pl.pallas_call(functools.partial(kernel, sizes), out_shape=(jax.ShapeDtyp...  67.7 us
    pallas_call x1, Pallas kernels, body(): pl.pallas_call(finish, out_shape=(jax.ShapeDtypeStruct(raw, BF16), grad,...  2.54 us

profile of v4, /device:TPU:1, one launch (start us, length us, event | category | flops | bytes accessed | tf_op | source)
XLA Modules:
  0.0 70.9 jit_solution(17846519260261470227)
XLA Ops:
  0.6 67.7 %less_step.1 = (bf16[512,16,128]{2,1,0:T(8,128)(2,1)}, f32[8,16,128]{2,1,0:T(8,128)}, f32[8,16,128]{2,1,0:T(8,128)}) custom-call(bf16[512,16,128]{2,1,0:T(8,128)(2,1)} %bitcast.14, bf16[512,16,128]{2,1,0:T(8,128)(2,1)} %bitcast.15, bf16[512,16,128]{2,1,0:T(8,128)(2,1)} %bitcast.16, bf16[512,16,128]{2,1,0:T(8,128)(2,1)} %bitcast.17, s32[16,256]{1,0:T(8,128)} %bitcast.20, ...), custom_call_target="tpu_custom_call" | custom-call | tf_op jit(solution)/shard_map/less_step/pallas_call | solution.py:703
  68.4 2.5 %finish.1 = (bf16[512,16,128]{2,1,0:T(8,128)(2,1)}, f32[8,16,128]{2,1,0:T(8,128)}, f32[8,16,128]{2,1,0:T(8,128)}) custom-call(bf16[512,16,128]{2,1,0:T(8,128)(2,1)} %get-tuple-element.9.rows_hbm, f32[8,16,128]{2,1,0:T(8,128)} %get-tuple-element.10.gq_hbm, f32[8,16,128]{2,1,0:T(8,128)} %get-tuple-element.11.gk_hbm), custom_call_target="tpu_custom_call" | custom-call | tf_op jit(solution)/shard_map/finish/pallas_call | solution.py:718

commit v5 on v4

--- a/solution.py
+++ b/solution.py
@@ -146,7 +146,7 @@
     pl.semaphore_wait(barrier, 2 + group - 1 + nz - 1 + nx - 1)
     halo_copies = []
     for n, (a, first, count) in enumerate(HALO_PIECES):
-        source = (k_hbm, v_hbm)[a].at[pl.ds(tokens - TILE + first, count)]
+        source = (k_raw, v_raw)[a].at[pl.ds(tokens - TILE + first, count)]
         target = halo_raw.at[a, pl.ds(first, count)]
         halo_copies.append(remote(source, target, halo_sems.at[0, n], halo_sems.at[1, n], after))
     halo_copies[0].start()
@@ -227,13 +227,18 @@
         lax.fori_loop(0, group // 2 // steps, one, 0)
         land[me] = buffer[me]
 
+    at_lane = [
+        (lanes == lax.broadcasted_iota(jnp.int32, (8, TILE), 0) + 8 * i).astype(F32)
+        for i in range(own)
+    ]
+
     def owner_slice(pieces, norms):
-        low = jnp.where(lanes < TILE // 2, norms[0], norms[1])
-        return jnp.concatenate([*pieces, low], 0)
-
-    def norm_of(tile, i):
-        turned = pltpu.roll(tile, TILE // 2, 1)
-        return jnp.where(lanes < TILE // 2, *((tile, turned) if i == 0 else (turned, tile)))
+        spread = sum(norms[i] * at_lane[i] for i in range(1, own)) + norms[0] * at_lane[0]
+        return jnp.concatenate([*pieces, jnp.sum(spread, 0, keepdims=True)], 0)
+
+    def norm_of(row, i):
+        picked = jnp.sum(row * at_lane[i], 1, keepdims=True)
+        return jnp.broadcast_to(picked, (8, TILE))
 
     own_rows = pl.ds(TILE, tokens)
 
@@ -658,7 +663,7 @@
     own = heads // group
     ext = tokens + TILE
     part = (own * rank, width)
-    slab = (own * rank + 8, width)
+    slab = (own * rank + 1, width)
     dma = pltpu.SemaphoreType.DMA
 
     def vmem(shape, dtype=F32):

time: 71 us -> 69.7 us (0.982)
  Pallas kernels: 70.3 us -> 69 us
    pallas_call x1, Pallas kernels: 67.7 us -> 66.5 us  [body(): pl.pallas_call(functools.partial(kernel, sizes), out_shape=(jax.ShapeDtyp...]
where the time goes in v5:
time: 69.7 us; the launch traced here: 69.6 us
  Pallas kernels  69 us (99%)
    pallas_call x1, Pallas kernels, body(): pl.pallas_call(functools.partial(kernel, sizes), out_shape=(jax.ShapeDtyp...  66.5 us
    pallas_call x1, Pallas kernels, body(): pl.pallas_call(finish, out_shape=(jax.ShapeDtypeStruct(raw, BF16), grad,...  2.54 us

profile of v5, /device:TPU:1, one launch (start us, length us, event | category | flops | bytes accessed | tf_op | source)
XLA Modules:
  0.0 69.6 jit_solution(14244413885706810406)
XLA Ops:
  0.6 66.5 %less_step.1 = (bf16[512,16,128]{2,1,0:T(8,128)(2,1)}, f32[8,16,128]{2,1,0:T(8,128)}, f32[8,16,128]{2,1,0:T(8,128)}) custom-call(bf16[512,16,128]{2,1,0:T(8,128)(2,1)} %bitcast.14, bf16[512,16,128]{2,1,0:T(8,128)(2,1)} %bitcast.15, bf16[512,16,128]{2,1,0:T(8,128)(2,1)} %bitcast.16, bf16[512,16,128]{2,1,0:T(8,128)(2,1)} %bitcast.17, s32[16,256]{1,0:T(8,128)} %bitcast.20, ...), custom_call_target="tpu_custom_call" | custom-call | tf_op jit(solution)/shard_map/less_step/pallas_call | solution.py:708
  67.1 2.5 %finish.1 = (bf16[512,16,128]{2,1,0:T(8,128)(2,1)}, f32[8,16,128]{2,1,0:T(8,128)}, f32[8,16,128]{2,1,0:T(8,128)}) custom-call(bf16[512,16,128]{2,1,0:T(8,128)(2,1)} %get-tuple-element.9.rows_hbm, f32[8,16,128]{2,1,0:T(8,128)} %get-tuple-element.10.gq_hbm, f32[8,16,128]{2,1,0:T(8,128)} %get-tuple-element.11.gk_hbm), custom_call_target="tpu_custom_call" | custom-call | tf_op jit(solution)/shard_map/finish/pallas_call | solution.py:723

commit v6 on v5

--- a/solution.py
+++ b/solution.py
@@ -526,8 +526,6 @@
 
     others(lambda s: arrival(rq_send, rq_land, rq_sems[0], s).wait_recv())
     rq_z[...] = sum(rq_land[s] for s in range(1, group)) + rq_land[0]
-    others(lambda t: z_copy(rq_z, rq_zland, rq_sems[1], t).start(), nz, z)
-    rq_zland[z] = rq_z[...]
 
     lax.fori_loop(0, 4, outputs_owner, 0)
 
@@ -544,11 +542,9 @@
         running = running + s_land[s]
     others(lambda s: scatter(s_out, s_back, s_sems[2], s).start())
     s_back[me] = s_out[me]
-
-    others(lambda t: z_arrival(rq_z, rq_zland, rq_sems[1], t).wait_recv(), nz, z)
-    rq_x[...] = sum(rq_zland[t] for t in range(1, nz)) + rq_zland[0]
-    others(lambda t: x_copy(rq_x, rq_xland, rq_sems[2], t).start(), nx, x)
-    rq_xland[x] = rq_x[...]
+    others(lambda t: z_copy(rq_z, rq_zland, rq_sems[1], t).start(), nz, z)
+    rq_zland[z] = rq_z[...]
+
 
     lax.fori_loop(4, 6, outputs_owner, 0)
 
@@ -568,12 +564,11 @@
 
     each_owner(key_products, lambda o: arrival(s_out, s_back, s_sems[2], o).wait_recv())
     by_owner(key_slice, rk_send, rk_land, rk_sems[0], 2)
-
-    others(lambda t: x_arrival(rq_x, rq_xland, rq_sems[2], t).wait_recv(), nx, x)
-    rq_sum[...] = sum(rq_xland[t] for t in range(1, nx)) + rq_xland[0]
-    others(lambda s: share(rq_sum, gq_hbm, rq_sems[3], s).start())
-    own_gq = pltpu.make_async_copy(rq_sum, gq_hbm.at[me], store_sem.at[tiles])
-    own_gq.start()
+    others(lambda t: z_arrival(rq_z, rq_zland, rq_sems[1], t).wait_recv(), nz, z)
+    rq_x[...] = sum(rq_zland[t] for t in range(1, nz)) + rq_zland[0]
+    others(lambda t: x_copy(rq_x, rq_xland, rq_sems[2], t).start(), nx, x)
+    rq_xland[x] = rq_x[...]
+
 
     lax.fori_loop(6, group, outputs_owner, 0)
 
@@ -597,6 +592,11 @@
     rk_z[...] = sum(rk_land[s] for s in range(1, group)) + rk_land[0]
     others(lambda t: z_copy(rk_z, rk_zland, rk_sems[1], t).start(), nz, z)
     rk_zland[z] = rk_z[...]
+    others(lambda t: x_arrival(rq_x, rq_xland, rq_sems[2], t).wait_recv(), nx, x)
+    rq_sum[...] = sum(rq_xland[t] for t in range(1, nx)) + rq_xland[0]
+    others(lambda s: share(rq_sum, gq_hbm, rq_sems[3], s).start())
+    own_gq = pltpu.make_async_copy(rq_sum, gq_hbm.at[me], store_sem.at[tiles])
+    own_gq.start()
     for t in range(1, tiles):
         store(t)
     others(lambda t: z_arrival(rk_z, rk_zland, rk_sems[1], t).wait_recv(), nz, z)

time: 69.7 us -> 68.9 us (0.989)
  Pallas kernels: 69 us -> 68.1 us
    pallas_call x1, Pallas kernels: 66.5 us -> 65.6 us  [body(): pl.pallas_call(functools.partial(kernel, sizes), out_shape=(jax.ShapeDtyp...]
where the time goes in v6:
time: 68.9 us; the launch traced here: 68.7 us
  Pallas kernels  68.1 us (99%)
    pallas_call x1, Pallas kernels, body(): pl.pallas_call(functools.partial(kernel, sizes), out_shape=(jax.ShapeDtyp...  65.6 us
    pallas_call x1, Pallas kernels, body(): pl.pallas_call(finish, out_shape=(jax.ShapeDtypeStruct(raw, BF16), grad,...  2.54 us

profile of v6, /device:TPU:1, one launch (start us, length us, event | category | flops | bytes accessed | tf_op | source)
XLA Modules:
  0.0 68.7 jit_solution(4239485578811471044)
XLA Ops:
  0.6 65.6 %less_step.1 = (bf16[512,16,128]{2,1,0:T(8,128)(2,1)}, f32[8,16,128]{2,1,0:T(8,128)}, f32[8,16,128]{2,1,0:T(8,128)}) custom-call(bf16[512,16,128]{2,1,0:T(8,128)(2,1)} %bitcast.14, bf16[512,16,128]{2,1,0:T(8,128)(2,1)} %bitcast.15, bf16[512,16,128]{2,1,0:T(8,128)(2,1)} %bitcast.16, bf16[512,16,128]{2,1,0:T(8,128)(2,1)} %bitcast.17, s32[16,256]{1,0:T(8,128)} %bitcast.20, ...), custom_call_target="tpu_custom_call" | custom-call | tf_op jit(solution)/shard_map/less_step/pallas_call | solution.py:708
  66.2 2.5 %finish.1 = (bf16[512,16,128]{2,1,0:T(8,128)(2,1)}, f32[8,16,128]{2,1,0:T(8,128)}, f32[8,16,128]{2,1,0:T(8,128)}) custom-call(bf16[512,16,128]{2,1,0:T(8,128)(2,1)} %get-tuple-element.9.rows_hbm, f32[8,16,128]{2,1,0:T(8,128)} %get-tuple-element.10.gq_hbm, f32[8,16,128]{2,1,0:T(8,128)} %get-tuple-element.11.gk_hbm), custom_call_target="tpu_custom_call" | custom-call | tf_op jit(solution)/shard_map/finish/pallas_call | solution.py:723
